TPU v7x, 32 devices: a whole 2x2x4 slice. The times are simulated.
32 devices in a mesh: groups: 2 (over y), ctx: 4 (over z), head: 2 (over x), feat: 2 (over core).
Axes of the slice: x: 2, y: 2, z: 4, core: 2. Of those that a mesh axis runs over, the one named last changes fastest.
Arguments:
- queries: bfloat16 [1024, 5120], P(('groups', 'ctx'), 'head'), parts along dimension 0, may hold values from -6 to 6
- keys: bfloat16 [1024, 1024], P(('groups', 'ctx'), 'head'), parts along dimension 0, may hold values from -6 to 6
- values: bfloat16 [1024, 1024], P(('groups', 'ctx'), 'head'), parts along dimension 0, may hold values from -6 to 6
- log_gate: float32 [1024, 8], P(('groups', 'ctx'), 'head'), parts along dimension 0, may hold values from -1 to 0, as said below
- cand_q: bfloat16 [128, 5120], P('groups', 'head'), parts along dimension 0, may hold values from -12 to 12
- cand_kv: bfloat16 [128, 2, 1024], P('groups', None, 'head'), parts along dimension 0, may hold values from -12 to 12
- token_ids: int32 [32], P('groups'), parts along dimension 0, may hold values from 0 to 63
- fork_pos: int32 [32], P('groups'), parts along dimension 0, may hold values from 1 to 4
- slot_map: int32 [32], P('groups'), parts along dimension 0, may hold values from 0 to 15, each once
Outputs:
- prefill_out: bfloat16 [1024, 5120], P(('groups', 'ctx', 'feat'), 'head'), parts along dimension 0
- branch_out: bfloat16 [32, 5120], P(('groups', 'ctx', 'feat'), 'head'), parts along dimension 0
There are 2 independent parts, one for each index of `groups`. A program takes and returns all parts, laid end to end along the dimension named above; each array names one. Nothing has to cross between parts.
Inputs may be any that keep to these rules, and one draw needn't show every extreme that they name: log_gate is never positive.
All inputs are finite; a program needn't handle non-finite values.
Results may differ from a plain program's by a relative error of at most 0.0055.
Values may be sent and summed in bfloat16 or wider, within the bound.
No kernel may reach another device: no remote copies, remote signals or barrier semaphores. Data moves between devices by JAX's collectives and lax.ppermute only.
A program may use at most 192 MiB of HBM per device.

v0:
```python
import math

import jax
import jax.numpy as jnp
from jax import lax
from jax.sharding import PartitionSpec as P

HEAD = 128
GROUP = 5


def carried_in(shard, axis, combine, identity):
    count, mine = (lax.axis_size(axis), lax.axis_index(axis))
    everything = jax.tree.map(lambda part: lax.all_gather(part, axis), shard)
    start = jax.tree.map(
        lambda part, zero: jnp.broadcast_to(jnp.asarray(zero, part.dtype), part.shape),
        shard,
        identity,
    )

    def step(k, before):
        reached = k < mine
        new = combine(before, jax.tree.map(lambda part: part[k], everything))
        return jax.tree.map(lambda a, b: jnp.where(reached, a, b), new, before)

    return lax.fori_loop(0, count, step, start)


def expand_part(block, parity):
    wide = block.astype(jnp.float32)
    rows = wide.shape[0]
    width = wide.shape[1]
    quarter = width // 4
    doubled = jnp.concatenate([wide, wide], axis=1)
    shifted = lax.dynamic_slice_in_dim(doubled, parity, 2 * width - 1, 1)
    partner = jnp.stack(
        [shifted[:, 2 * step : 2 * step + width] for step in range(quarter)], axis=1
    )
    offsets = parity + 2 * lax.broadcasted_iota(jnp.int32, (quarter,), 0)
    weight = jnp.where(offsets == 0, 1.0, math.sqrt(2.0)).astype(jnp.float32)
    bulk = (wide[:, None, :] * partner * weight[None, :, None]).reshape(rows, quarter * width)
    lower = lax.dynamic_slice_in_dim(wide, parity * quarter, quarter, 1)
    upper = lax.dynamic_slice_in_dim(wide, parity * quarter + width // 2, quarter, 1)
    tail = lower * upper * math.sqrt(2.0)
    return jnp.concatenate([bulk, tail], axis=1).astype(jnp.bfloat16)


def chain_combine(earlier, later):
    decay = earlier[0] * later[0]
    states = later[0][:, None, None] * earlier[1] + later[1]
    norms = later[0][:, None] * earlier[2] + later[2]
    return (decay, states, norms)


def per_device(queries, keys, values, log_gate, cand_q, cand_kv, token_ids, fork_pos, slot_map):
    feat_count = lax.axis_size("feat")
    feat_index = lax.axis_index("feat")
    ctx_index = lax.axis_index("ctx")
    length = queries.shape[0]
    kv_local = keys.shape[1] // HEAD
    cumul = jnp.cumsum(log_gate, axis=0)
    finals = cumul[-1]
    carry_w = jnp.exp(finals[None, :] - cumul)
    state_list = []
    norm_list = []
    for head in range(kv_local):
        key_h = keys[:, head * HEAD : (head + 1) * HEAD]
        value_h = values[:, head * HEAD : (head + 1) * HEAD]
        phik = expand_part(key_h, feat_index)
        scaled = (carry_w[:, head : head + 1] * value_h.astype(jnp.float32)).astype(jnp.bfloat16)
        state_list.append(
            lax.dot_general(
                phik, scaled, (((0,), (0,)), ((), ())), preferred_element_type=jnp.float32
            )
        )
        norm_list.append(
            jnp.dot(carry_w[:, head].astype(jnp.bfloat16), phik, preferred_element_type=jnp.float32)
        )
    local_states = jnp.stack(state_list)
    local_norms = jnp.stack(norm_list)
    decays = jnp.exp(finals)
    identity = (jnp.ones_like(decays), jnp.zeros_like(local_states), jnp.zeros_like(local_norms))
    scanned = carried_in((decays, local_states, local_norms), "ctx", chain_combine, identity)
    prior_states = scanned[1]
    prior_norms = scanned[2]
    prior_sb = prior_states.astype(jnp.bfloat16)
    prior_zb = prior_norms.astype(jnp.bfloat16)
    part_rows = length // feat_count
    row_start = feat_index * part_rows
    own_q = lax.dynamic_slice_in_dim(queries, row_start, part_rows, 0)
    own_cum = lax.dynamic_slice_in_dim(cumul, row_start, part_rows, 0)
    inter_num = []
    inter_den = []
    for head in range(kv_local):
        growth = jnp.exp(cumul[:, head])
        for member in range(GROUP):
            column = (head * GROUP + member) * HEAD
            phiq = expand_part(queries[:, column : column + HEAD], feat_index)
            inter_num.append(
                jnp.dot(phiq, prior_sb[head], preferred_element_type=jnp.float32)
                * growth[:, None]
                / HEAD
            )
            inter_den.append(
                jnp.dot(phiq, prior_zb[head], preferred_element_type=jnp.float32) * growth / HEAD
            )
    summed_num, summed_den = (
        lax.psum_scatter(
            jnp.concatenate(inter_num, axis=1), "feat", scatter_dimension=0, tiled=True
        ),
        lax.psum_scatter(jnp.stack(inter_den, axis=1), "feat", scatter_dimension=0, tiled=True),
    )
    row_pos = row_start + lax.broadcasted_iota(jnp.int32, (part_rows, length), 0)
    col_pos = lax.broadcasted_iota(jnp.int32, (part_rows, length), 1)
    causal = col_pos <= row_pos
    prefill_pieces = []
    for head in range(kv_local):
        key_h = keys[:, head * HEAD : (head + 1) * HEAD]
        value_h = values[:, head * HEAD : (head + 1) * HEAD]
        spread = own_cum[:, head][:, None] - cumul[:, head][None, :]
        fading = jnp.where(causal, jnp.exp(jnp.where(causal, spread, 0.0)), 0.0)
        for member in range(GROUP):
            index = head * GROUP + member
            raw = lax.dot_general(
                own_q[:, index * HEAD : (index + 1) * HEAD],
                key_h,
                (((1,), (1,)), ((), ())),
                preferred_element_type=jnp.float32,
            )
            weights = raw * raw / HEAD * fading
            numer = summed_num[:, index * HEAD : (index + 1) * HEAD] + jnp.dot(
                weights.astype(jnp.bfloat16), value_h, preferred_element_type=jnp.float32
            )
            denom = summed_den[:, index] + jnp.sum(weights, axis=1)
            prefill_pieces.append((numer / jnp.maximum(denom, 1.0)[:, None]).astype(jnp.bfloat16))
    prefill_out = jnp.concatenate(prefill_pieces, axis=1)
    branches = token_ids.shape[0]
    order = (slot_map[None, :] == lax.broadcasted_iota(jnp.int32, (branches, branches), 0)).astype(
        jnp.int32
    )
    ids_sorted = jnp.sum(order * token_ids[None, :], axis=1)
    fork_sorted = jnp.sum(order * fork_pos[None, :], axis=1)
    pick = (
        ids_sorted[:, None] == lax.broadcasted_iota(jnp.int32, (branches, cand_q.shape[0]), 1)
    ).astype(jnp.bfloat16)
    new_q = jnp.dot(pick, cand_q, preferred_element_type=jnp.float32).astype(jnp.bfloat16)
    new_kv = jnp.einsum("bc,cpd->bpd", pick, cand_kv, preferred_element_type=jnp.float32).astype(
        jnp.bfloat16
    )
    included_states = decays[:, None, None] * prior_states + local_states
    included_norms = decays[:, None] * prior_norms + local_norms
    dnum_list = []
    dden_list = []
    chosen = (fork_sorted - 1 == ctx_index).astype(jnp.float32)
    for head in range(kv_local):
        state_b = included_states[head].astype(jnp.bfloat16)
        norm_b = included_norms[head].astype(jnp.bfloat16)
        for member in range(GROUP):
            column = (head * GROUP + member) * HEAD
            phiq = expand_part(new_q[:, column : column + HEAD], feat_index)
            dnum_list.append(
                jnp.dot(phiq, state_b, preferred_element_type=jnp.float32) * chosen[:, None] / HEAD
            )
            dden_list.append(
                jnp.dot(phiq, norm_b, preferred_element_type=jnp.float32) * chosen / HEAD
            )
    total_num, total_den = (
        lax.psum_scatter(
            jnp.concatenate(dnum_list, axis=1), ("ctx", "feat"), scatter_dimension=0, tiled=True
        ),
        lax.psum_scatter(
            jnp.stack(dden_list, axis=1), ("ctx", "feat"), scatter_dimension=0, tiled=True
        ),
    )
    owned = total_num.shape[0]
    first = (ctx_index * feat_count + feat_index) * owned
    mine_q = lax.dynamic_slice_in_dim(new_q, first, owned, 0)
    mine_kv = lax.dynamic_slice_in_dim(new_kv, first, owned, 0)
    branch_pieces = []
    for head in range(kv_local):
        key_n = mine_kv[:, 0, head * HEAD : (head + 1) * HEAD].astype(jnp.float32)
        value_n = mine_kv[:, 1, head * HEAD : (head + 1) * HEAD].astype(jnp.float32)
        for member in range(GROUP):
            index = head * GROUP + member
            query_n = mine_q[:, index * HEAD : (index + 1) * HEAD].astype(jnp.float32)
            inner = jnp.sum(query_n * key_n, axis=1)
            own_weight = inner * inner / HEAD
            numer = total_num[:, index * HEAD : (index + 1) * HEAD] + own_weight[:, None] * value_n
            denom = total_den[:, index] + own_weight
            branch_pieces.append((numer / jnp.maximum(denom, 1.0)[:, None]).astype(jnp.bfloat16))
    branch_out = jnp.concatenate(branch_pieces, axis=1)
    return (prefill_out, branch_out)


def solution(mesh):
    return jax.shard_map(
        per_device,
        mesh=mesh,
        in_specs=(
            P(("groups", "ctx"), "head"),
            P(("groups", "ctx"), "head"),
            P(("groups", "ctx"), "head"),
            P(("groups", "ctx"), "head"),
            P("groups", "head"),
            P("groups", None, "head"),
            P("groups"),
            P("groups"),
            P("groups"),
        ),
        out_specs=(P(("groups", "ctx", "feat"), "head"), P(("groups", "ctx", "feat"), "head")),
        check_vma=False,
    )
```

profile of v0, /device:TPU:0, one launch (start us, length us, event | category | flops | bytes accessed | tf_op | source)
XLA Modules:
  0.0 848.2 jit_solution(6095518286896023935)
XLA Ops:
  49.0 21.1 %fusion.3 = (bf16[128,4096]{0,1:T(8,128)(2,1)}, bf16[128,4096]{0,1:T(8,128)(2,1)}, bf16[128,4096]{0,1:T(8,128)(2,1)}, bf16[128,4096]{0,1:T(8,128)(2,1)}, bf16[12...) fusion(f32[128,32,128]{0,2,1:T(8,128)} %broadcast_multiply_fusi, ...), kind=kLoop, calls=%fused_computation.1502 | loop fusion | flops 18874368 | bytes 56639488 | tf_op jit(solution)/shard_map/convert.56
  76.3 3.5 pad_maximum_fusion
  79.8 2.4 fusion.267
  82.2 2.3 fusion.268
  110.6 46.5 %all-gather.3 = f32[4,4,4128]{2,1,0:T(4,128)S(1)} all-gather(f32[1,4,4128]{2,1,0:T(4,128)S(1)} %fusion.453), channel_id=3, replica_groups=mesh['groups'=2,'ctx'=4,'head'=2,'feat'=2] {'ctx'}, dimensions={0}, use_global_device_ids=true | all-gather | bytes 330240 | tf_op jit(solution)/shard_map/all_gather | solution.py:14
  157.2 9.4 %all-gather.2 = f32[4,1,4]{2,1,0:T(1,128)} all-gather(f32[1,1,4]{2,1,0:T(1,128)} %get-tuple-element.261), channel_id=1, replica_groups=mesh['groups'=2,'ctx'=4,'head'=2,'feat'=2] {'ctx'}, dimensions={0}, use_global_device_ids=true | all-gather | bytes 80 | tf_op jit(solution)/shard_map/all_gather | solution.py:14
  215.8 2.2 fusion.800
  218.0 2.2 fusion.801
  224.4 2.2 fusion.804
  226.6 2.2 fusion.805
  230.9 2.2 fusion.807
  235.3 2.2 fusion.809
  237.5 2.2 fusion.810
  261.1 2.2 fusion.813
  263.3 2.2 fusion.814
  265.5 2.2 fusion.815
  269.7 2.2 fusion.817
  271.9 2.2 fusion.818
  274.1 2.2 fusion.819
  279.3 9.8 %constant_dynamic-update-slice_fusion.717 = f32[128,32,128]{0,2,1:T(8,128)S(1)} fusion(f32[128,32,128]{0,2,1:T(8,128)S(1)} %constant_dynamic-update-slice_fusion.718, f32[128,255]{0,1:T(8,128)S(1)} %get-tuple-element.430), kind=kLoop, calls=%fused_computation.730 | loop fusion | bytes 131072
  295.0 4.1 fusion.4
  299.1 355.2 %all-gather.6.cloned.1.call-done = f32[16,4128,128]{2,1,0:T(8,128)} async-done(((f32[4,4128,128]{2,1,0:T(8,128)}), f32[16,4128,128]{2,1,0:T(8,128)}) %all-gather.6.cloned.1.call-update) | async-done | bytes 33816592 | tf_op jit(solution)/shard_map/all_gather | solution.py:14
  654.3 42.2 %while.16 = (s32[]{:T(128)}, f32[4,4128,128]{2,1,0:T(8,128)}, f32[4,4128]{1,0:T(4,128)S(1)}, s32[]{:T(128)}, f32[4,4]{1,0:T(4,128)}, /*index=5*/f32[4,4,4128,128...) while((s32[]{:T(128)}, f32[4,4128,128]{2,1,0:T(8,128)}, f32[4,4128]{1,0:T(4,128)S(1)}, ...), condition=%wide.region_2.3_spmd.clone, body=%wide.region_1.2_spmd.clone.sunk | while | flops 8520196 | bytes 25560768 | solution.py:26
  655.0 7.8 fusion.845
  663.7 10.3 %fusion.845 = f32[4,4128,128]{2,1,0:T(8,128)} fusion(f32[4,4,4128,128]{3,2,1,0:T(8,128)} %get-tuple-element.597, s32[]{:T(128)} %get-tuple-element.583, f32[4,4128,128]{2,1,0:T(8,128)} %get-tuple-element.584, f32[4]{0:T(128)S(1)} %fusion.844, pred[]{:T(512)S(6)} %compare.3, pred[]{:T(512)S(6)} %lt.38), kind=kLoop, calls=%fused_computation.1.clone.1 | loop fusion | flops 8454144 | bytes 25362454 | tf_op jit(solution)/shard_map/while/body/eval_jaxpr/jit(_where)/select_n | solution.py:24
  674.8 10.3 %fusion.845 = f32[4,4128,128]{2,1,0:T(8,128)} fusion(f32[4,4,4128,128]{3,2,1,0:T(8,128)} %get-tuple-element.597, s32[]{:T(128)} %get-tuple-element.583, f32[4,4128,128]{2,1,0:T(8,128)} %get-tuple-element.584, f32[4]{0:T(128)S(1)} %fusion.844, pred[]{:T(512)S(6)} %compare.3, pred[]{:T(512)S(6)} %lt.38), kind=kLoop, calls=%fused_computation.1.clone.1 | loop fusion | flops 8454144 | bytes 25362454 | tf_op jit(solution)/shard_map/while/body/eval_jaxpr/jit(_where)/select_n | solution.py:24
  685.9 10.5 %fusion.845 = f32[4,4128,128]{2,1,0:T(8,128)} fusion(f32[4,4,4128,128]{3,2,1,0:T(8,128)} %get-tuple-element.597, s32[]{:T(128)} %get-tuple-element.583, f32[4,4128,128]{2,1,0:T(8,128)} %get-tuple-element.584, f32[4]{0:T(128)S(1)} %fusion.844, pred[]{:T(512)S(6)} %compare.3, pred[]{:T(512)S(6)} %lt.38), kind=kLoop, calls=%fused_computation.1.clone.1 | loop fusion | flops 8454144 | bytes 25362454 | tf_op jit(solution)/shard_map/while/body/eval_jaxpr/jit(_where)/select_n | solution.py:24
  696.7 10.6 %add_convert_fusion = (bf16[4,4128,128]{2,1,0:T(8,128)(2,1)S(1)}, bf16[4,4128,128]{2,1,0:T(8,128)(2,1)}) fusion(f32[4,4128,128]{2,1,0:T(8,128)} %get-tuple-element.127, f32[4]{0:T(128)S(1)} %copy-done.227, f32[1,4128,128]{2,1,0:T(8,128)} %copy-done.4, f32[1,4128,128]{2,1,0:T(8,128)S(1)} %convolution_bitcast_fusion.1, f32[1,4128,128]{2,1,0:T(8,128)} %copy-done.2, ...), kind=kLoop, calls=%fused_computation.7 | loop fusion | flops 14794752 | bytes 25362448 | tf_op jit(solution)/shard_map/convert.53
  728.9 2.2 constant_dynamic-update-slice_fusion.787
  755.1 26.9 %all-reduce.1 = f32[16,20]{0,1:T(8,128)S(1)} all-reduce(f32[16,20]{0,1:T(8,128)S(1)} %stack.6015), channel_id=7, replica_groups=mesh['groups'=2,'ctx'=4,'head'=2,'feat'=2] {'ctx','feat'}, use_global_device_ids=true, to_apply=%region_29.30.clone | all-reduce | flops 320 | bytes 2560
  782.7 2.2 fusion.799
  800.2 6.6 all-reduce.4.cloned.1.call-done
  (2343 shorter events, 253.1 us)
Async XLA Ops:
  7.2 80.5 %copy-start = (bf16[64,2560]{1,0:T(8,128)(2,1)S(1)}, bf16[64,2560]{1,0:T(8,128)(2,1)}, u32[]{:S(2)}) copy-start(bf16[64,2560]{1,0:T(8,128)(2,1)} %param.15) | copy-start | bytes 983044
  7.2 647.1 %all-gather.6.cloned.1.call-start = ((), (), s32[]{:S(2)}) async-start(), calls=%async_computation.2 | async-start | bytes 42270720 | tf_op jit(solution)/shard_map/all_gather | solution.py:14
  79.8 702.9 %reduce-scatter.10.cloned.1.call-start = ((), (), s32[]{:S(2)}) async-start(), calls=%async_computation.4 | async-start | bytes 98304
  728.6 78.1 %all-reduce.4.cloned.1.call-start = ((), (), s32[]{:S(2)}) async-start(), calls=%async_computation.5 | async-start | bytes 327680
  754.6 52.1 %copy-start.232 = (f32[2]{0:T(128)S(1)}, f32[2]{0:T(128)}, u32[]{:S(2)}) copy-start(f32[2]{0:T(128)} %get-tuple-element.480) | copy-start | bytes 28
  754.6 53.7 %copy-start.251 = (f32[2]{0:T(128)S(1)}, f32[2]{0:T(128)}, u32[]{:S(2)}) copy-start(f32[2]{0:T(128)} %get-tuple-element.490) | copy-start | bytes 28
  754.6 54.5 %copy-start.250 = (f32[2]{0:T(128)S(1)}, f32[2]{0:T(128)}, u32[]{:S(2)}) copy-start(f32[2]{0:T(128)} %get-tuple-element.489) | copy-start | bytes 28
  754.6 55.2 %copy-start.249 = (f32[2]{0:T(128)S(1)}, f32[2]{0:T(128)}, u32[]{:S(2)}) copy-start(f32[2]{0:T(128)} %get-tuple-element.488) | copy-start | bytes 28
  754.6 56.0 %copy-start.248 = (f32[2]{0:T(128)S(1)}, f32[2]{0:T(128)}, u32[]{:S(2)}) copy-start(f32[2]{0:T(128)} %get-tuple-element.487) | copy-start | bytes 28
  754.6 56.8 %copy-start.247 = (f32[2]{0:T(128)S(1)}, f32[2]{0:T(128)}, u32[]{:S(2)}) copy-start(f32[2]{0:T(128)} %get-tuple-element.486) | copy-start | bytes 28
  754.6 57.6 %copy-start.246 = (f32[2]{0:T(128)S(1)}, f32[2]{0:T(128)}, u32[]{:S(2)}) copy-start(f32[2]{0:T(128)} %get-tuple-element.485) | copy-start | bytes 28
  754.6 58.3 %copy-start.245 = (f32[2]{0:T(128)S(1)}, f32[2]{0:T(128)}, u32[]{:S(2)}) copy-start(f32[2]{0:T(128)} %get-tuple-element.484) | copy-start | bytes 28
  754.7 59.1 %copy-start.244 = (f32[2]{0:T(128)S(1)}, f32[2]{0:T(128)}, u32[]{:S(2)}) copy-start(f32[2]{0:T(128)} %get-tuple-element.483) | copy-start | bytes 28
  754.7 59.9 %copy-start.243 = (f32[2]{0:T(128)S(1)}, f32[2]{0:T(128)}, u32[]{:S(2)}) copy-start(f32[2]{0:T(128)} %get-tuple-element.482) | copy-start | bytes 28
  754.7 60.6 %copy-start.242 = (f32[2]{0:T(128)S(1)}, f32[2]{0:T(128)}, u32[]{:S(2)}) copy-start(f32[2]{0:T(128)} %get-tuple-element.481) | copy-start | bytes 28
  754.7 61.4 %copy-start.237 = (f32[2]{0:T(128)S(1)}, f32[2]{0:T(128)}, u32[]{:S(2)}) copy-start(f32[2]{0:T(128)} %get-tuple-element.479) | copy-start | bytes 28
  754.7 62.2 %copy-start.241 = (f32[2]{0:T(128)S(1)}, f32[2]{0:T(128)}, u32[]{:S(2)}) copy-start(f32[2]{0:T(128)} %get-tuple-element.478) | copy-start | bytes 28
  754.7 63.0 %copy-start.240 = (f32[2]{0:T(128)S(1)}, f32[2]{0:T(128)}, u32[]{:S(2)}) copy-start(f32[2]{0:T(128)} %get-tuple-element.477) | copy-start | bytes 28
  754.7 63.7 %copy-start.239 = (f32[2]{0:T(128)S(1)}, f32[2]{0:T(128)}, u32[]{:S(2)}) copy-start(f32[2]{0:T(128)} %get-tuple-element.476) | copy-start | bytes 28
  754.7 64.5 %copy-start.238 = (f32[2]{0:T(128)S(1)}, f32[2]{0:T(128)}, u32[]{:S(2)}) copy-start(f32[2]{0:T(128)} %get-tuple-element.475) | copy-start | bytes 28
  754.7 65.3 %copy-start.236 = (f32[2]{0:T(128)S(1)}, f32[2]{0:T(128)}, u32[]{:S(2)}) copy-start(f32[2]{0:T(128)} %get-tuple-element.474) | copy-start | bytes 28
  754.7 66.1 %copy-start.235 = (f32[2]{0:T(128)S(1)}, f32[2]{0:T(128)}, u32[]{:S(2)}) copy-start(f32[2]{0:T(128)} %get-tuple-element.473) | copy-start | bytes 28
  754.8 67.6 %copy-start.136 = (bf16[128,512]{1,0:T(8,128)(2,1)S(1)}, bf16[128,512]{1,0:T(8,128)(2,1)}, u32[]{:S(2)}) copy-start(bf16[128,512]{1,0:T(8,128)(2,1)} %param.13) | copy-start | bytes 393220
  754.8 67.6 %reduce-scatter.8.cloned.1.call-start = ((), (), s32[]{:S(2)}) async-start(), calls=%async_computation.3 | async-start | bytes 1966080 | tf_op jit(solution)/shard_map/reduce_scatter | solution.py:108
  782.6 50.6 %copy-start.280 = (bf16[64,128]{1,0:T(8,128)(2,1)S(1)}, bf16[64,128]{1,0:T(8,128)(2,1)}, u32[]{:S(2)}) copy-start(bf16[64,128]{1,0:T(8,128)(2,1)} %get-tuple-element.370) | copy-start | bytes 49156
  782.7 51.5 %copy-start.286 = (bf16[64,128]{1,0:T(8,128)(2,1)S(1)}, bf16[64,128]{1,0:T(8,128)(2,1)}, u32[]{:S(2)}) copy-start(bf16[64,128]{1,0:T(8,128)(2,1)} %get-tuple-element.372) | copy-start | bytes 49156
  784.9 51.1 %copy-start.287 = (bf16[64,128]{1,0:T(8,128)(2,1)S(1)}, bf16[64,128]{1,0:T(8,128)(2,1)}, u32[]{:S(2)}) copy-start(bf16[64,128]{1,0:T(8,128)(2,1)} %get-tuple-element.376) | copy-start | bytes 49156
  784.9 52.0 %copy-start.285 = (bf16[64,128]{1,0:T(8,128)(2,1)S(1)}, bf16[64,128]{1,0:T(8,128)(2,1)}, u32[]{:S(2)}) copy-start(bf16[64,128]{1,0:T(8,128)(2,1)} %get-tuple-element.378) | copy-start | bytes 49156
  785.8 51.9 %copy-start.283 = (bf16[64,128]{1,0:T(8,128)(2,1)S(1)}, bf16[64,128]{1,0:T(8,128)(2,1)}, u32[]{:S(2)}) copy-start(bf16[64,128]{1,0:T(8,128)(2,1)} %get-tuple-element.380) | copy-start | bytes 49156
  786.3 52.4 %copy-start.282 = (bf16[64,128]{1,0:T(8,128)(2,1)S(1)}, bf16[64,128]{1,0:T(8,128)(2,1)}, u32[]{:S(2)}) copy-start(bf16[64,128]{1,0:T(8,128)(2,1)} %get-tuple-element.382) | copy-start | bytes 49156
  786.7 52.9 %copy-start.281 = (bf16[64,128]{1,0:T(8,128)(2,1)S(1)}, bf16[64,128]{1,0:T(8,128)(2,1)}, u32[]{:S(2)}) copy-start(bf16[64,128]{1,0:T(8,128)(2,1)} %get-tuple-element.384) | copy-start | bytes 49156
  787.2 54.1 %copy-start.1 = (bf16[64,2560]{1,0:T(8,128)(2,1)S(1)}, bf16[64,2560]{1,0:T(8,128)(2,1)}, u32[]{:S(2)}) copy-start(bf16[64,2560]{1,0:T(8,128)(2,1)} %param.15) | copy-start | bytes 983044
  (263 other events, 2569.5 us)
Sparse Core Ops, SparseCore 0:
  79.9 574.3 all-gather.5
  728.7 6.5 reduce-scatter.9
  754.9 51.7 all-reduce.3
  808.8 10.2 reduce-scatter.7
where the time goes:
time: 863 us; the launch traced here: 848 us
  waiting for transfers between devices  362 us (42%)
  other arithmetic  171 us (20%)
  local copies, waits for them, and re-layouts  105 us (12%)
  matrix products  102 us (12%)
  blocking collectives  82.9 us (10%)
  between operations  25 us (3%)
    all_gather x1, waiting for transfers between devices, carried_in(): everything = jax.tree.map(lambda part: lax.all_gather(part, axis), shard)  355 us
    unnamed x1993, local copies, waits for them, and re-layouts  93.3 us
    all_gather x2, blocking collectives, carried_in(): everything = jax.tree.map(lambda part: lax.all_gather(part, axis), shard)  55.9 us
    another operation x28, other arithmetic  55.8 us
    dot_general x20, matrix products, per_device(): lax.dot_general(own_q[:, index * HEAD:(index + 1) * HEAD], key_h, (((1,),...  43.4 us
    select_n x8, other arithmetic, step(): return jax.tree.map(lambda a, b: jnp.where(reached, a, b), new, before)  39.4 us
    unnamed x1, blocking collectives  26.9 us
    mul x24, other arithmetic, expand_part(): wide[:, None, :] * partner * weight[None, :, None]  26.6 us
  transfers between devices with their start and end apart: 4, of which 2 were waited for; matrix products, arithmetic and copies ran while one was open for 24% of the time, Pallas kernels for 0%

commit v1 on v0

v1 whole, which is shorter than its diff:
```python
import functools

import jax
import jax.numpy as jnp
from jax import lax
from jax.experimental import pallas as pl
from jax.experimental.pallas import tpu as pltpu
from jax.sharding import PartitionSpec as P

HEAD = 128
GROUP = 5
GATE_ROWS = 16
MASKED = -1e30


def dot(a, b, contract, precision=None):
    return lax.dot_general(
        a, b, ((contract[:1], contract[1:]), ((), ())),
        precision=precision, preferred_element_type=jnp.float32,
    )


def exact_dot(a, b, contract):
    return dot(a, b, contract, lax.Precision.HIGHEST)


def gate_sums(log_gate):
    length = log_gate.shape[0]
    row = lax.broadcasted_iota(jnp.int32, (length, length), 0)
    col = lax.broadcasted_iota(jnp.int32, (length, length), 1)
    after = exact_dot(log_gate, (row > col).astype(jnp.float32), (0, 0))
    upto = exact_dot(log_gate, (row <= col).astype(jnp.float32), (0, 0))
    return after, upto


def split3(x):
    high = x.astype(jnp.bfloat16)
    rest = x - high.astype(jnp.float32)
    middle = rest.astype(jnp.bfloat16)
    low = (rest - middle.astype(jnp.float32)).astype(jnp.bfloat16)
    return [part.astype(jnp.float32) for part in (high, middle, low)]


def pack_kernel(k_ref, v_ref, g_ref, out_ref):
    length, width = k_ref.shape
    first_core = lax.axis_index("feat") == 0

    @pl.when(first_core)
    def _():
        out_ref[:length, :] = k_ref[...]

    @pl.when(jnp.logical_not(first_core))
    def _():
        out_ref[:length, :] = v_ref[...]

    after, upto = gate_sums(g_ref[...])
    place = lax.broadcasted_iota(jnp.int32, (GATE_ROWS, length), 0)
    for head in range(width // HEAD):
        total = jnp.broadcast_to(upto[head : head + 1, length - 1 :], (1, length))
        parts = split3(after[head : head + 1, :]) + split3(total)
        tile = jnp.zeros((GATE_ROWS, length), jnp.float32)
        for i, part in enumerate(parts):
            tile = jnp.where(place == i, part, tile)
        out_ref[length:, head * HEAD : (head + 1) * HEAD] = tile.astype(jnp.bfloat16)


def main_kernel(n_ctx, n_feat, partners, *refs):
    (q_ref, k_ref, v_ref, g_ref, cq_ref, ckv_ref, tok_ref, fork_ref, slot_ref) = refs[:9]
    near = refs[9 : 9 + len(partners)]
    far = refs[9 + len(partners) : 9 + 2 * len(partners)]
    out_ref, branch_ref, w_ref, value_ref, row_ref = refs[9 + 2 * len(partners) :]

    ctx = lax.axis_index("ctx")
    feat = lax.axis_index("feat")
    length, width = k_ref.shape
    heads = width // HEAD
    rows = out_ref.shape[0]
    owned = branch_ref.shape[0]
    padded = w_ref.shape[0] - GROUP * rows
    branches = tok_ref.shape[1]
    first_core = feat == 0
    start = pl.multiple_of(feat * rows, rows)
    blocks = [ctx] + [partner(ctx) for partner in partners]

    gate = g_ref[...]
    after, upto = gate_sums(gate)
    row = lax.broadcasted_iota(jnp.int32, (rows, length), 0) + start
    col = lax.broadcasted_iota(jnp.int32, (rows, length), 1)
    causal = col <= row
    row_sum = exact_dot(causal.astype(jnp.float32), gate, (1, 0))

    line = lax.broadcasted_iota(jnp.int32, (padded, 1), 0)
    slot = (ctx * n_feat + feat) * owned + lax.rem(line, owned)
    mine = slot_ref[...] == slot
    pick_id = jnp.sum(jnp.where(mine, tok_ref[...].astype(jnp.float32), 0.0), axis=1, keepdims=True)
    fork = jnp.sum(jnp.where(mine, fork_ref[...].astype(jnp.float32), 0.0), axis=1, keepdims=True)
    fork = fork.astype(jnp.int32)
    cands = cq_ref.shape[0]
    pick = (
        lax.broadcasted_iota(jnp.int32, (padded, cands), 1).astype(jnp.float32) == pick_id
    ).astype(jnp.bfloat16)

    value_ref[:, HEAD:] = jnp.ones((value_ref.shape[0], HEAD), jnp.bfloat16)
    scale = 1.0 / HEAD
    for head in range(heads):
        lanes = slice(head * HEAD, (head + 1) * HEAD)
        tails, totals, keys = [after[head : head + 1, :]], [], [k_ref[:, lanes]]
        totals.append(jnp.broadcast_to(upto[head : head + 1, length - 1 :], (1, length)))
        value_ref[:length, :HEAD] = v_ref[:, lanes]
        for i in range(len(partners)):
            part = near[i][length:, lanes].astype(jnp.float32)
            tails.append(part[0:1] + part[1:2] + part[2:3])
            totals.append(part[3:4] + part[4:5] + part[5:6])
            here, there = near[i][:length, lanes], far[i][:length, lanes]
            keys.append(jnp.where(first_core, here, there))
            value_ref[(i + 1) * length : (i + 2) * length, :HEAD] = jnp.where(
                first_core, there, here
            )

        picked = dot(pick, cq_ref[:, head * GROUP * HEAD : (head + 1) * GROUP * HEAD], (1, 0))
        branch_q = jnp.zeros((padded, HEAD), jnp.float32)
        for member in range(GROUP):
            chosen = (line >= member * owned) & (line < (member + 1) * owned)
            branch_q = jnp.where(chosen, picked[:, member * HEAD : (member + 1) * HEAD], branch_q)
        q_parts = [
            q_ref[pl.ds(start, rows), (head * GROUP + member) * HEAD : (head * GROUP + member + 1) * HEAD]
            for member in range(GROUP)
        ]
        q_all = jnp.concatenate(q_parts + [branch_q.astype(jnp.bfloat16)], axis=0)
        row_h = row_sum[:, head : head + 1]
        for b, block in enumerate(blocks):
            raw = dot(q_all, keys[b], (1, 1))
            square = raw * raw
            if b == 0:
                reach = jnp.where(causal, row_h - upto[head : head + 1, :], MASKED)
            else:
                between = jnp.zeros((1, length), jnp.float32)
                for o, other in enumerate(blocks):
                    if o not in (0, b):
                        inside = (other > block) & (other < ctx)
                        between = between + jnp.where(inside, totals[o], 0.0)
                reach = jnp.where(block < ctx, row_h + (between + tails[b]), MASKED)
            decay = jnp.exp(reach) * scale
            past = jnp.broadcast_to(tails[b], (padded, length))
            for o, other in enumerate(blocks):
                if o != b:
                    inside = (other > block) & (other < fork)
                    past = past + jnp.where(inside, totals[o], 0.0)
            branch_decay = jnp.exp(jnp.where(block < fork, past, MASKED)) * scale
            cols = slice(b * length, (b + 1) * length)
            for member in range(GROUP):
                span = slice(member * rows, (member + 1) * rows)
                w_ref[span, cols] = (square[span] * decay).astype(jnp.bfloat16)
            w_ref[GROUP * rows :, cols] = (square[GROUP * rows :] * branch_decay).astype(
                jnp.bfloat16
            )
        total = dot(w_ref[...], value_ref[...], (1, 0))
        prefill = total[: GROUP * rows]
        ratio = prefill[:, :HEAD] / jnp.maximum(prefill[:, HEAD:], 1.0)
        for member in range(GROUP):
            column = (head * GROUP + member) * HEAD
            out_ref[:, column : column + HEAD] = ratio[member * rows : (member + 1) * rows].astype(
                out_ref.dtype
            )
        new_k = dot(pick, ckv_ref[:, lanes], (1, 0))
        new_v = dot(pick, ckv_ref[:, width + head * HEAD : width + (head + 1) * HEAD], (1, 0))
        inner = jnp.sum(branch_q * new_k, axis=1, keepdims=True)
        own = inner * inner * scale
        branch = total[GROUP * rows :]
        row_ref[...] = (branch[:, :HEAD] + own * new_v) / jnp.maximum(branch[:, HEAD:] + own, 1.0)
        for member in range(GROUP):
            column = (head * GROUP + member) * HEAD
            branch_ref[:, column : column + HEAD] = row_ref[
                member * owned : (member + 1) * owned, :
            ].astype(branch_ref.dtype)


def swaps(count):
    if count & (count - 1) == 0:
        return [
            ([(i, i ^ step) for i in range(count)], functools.partial(lambda s, i: i ^ s, step))
            for step in range(1, count)
        ]
    return [
        (
            [(i, (i + step) % count) for i in range(count)],
            functools.partial(lambda s, i: lax.rem(i + count - s, count), step),
        )
        for step in range(1, count)
    ]


def per_device(queries, keys, values, log_gate, cand_q, cand_kv, token_ids, fork_pos, slot_map):
    n_ctx = lax.axis_size("ctx")
    n_feat = lax.axis_size("feat")
    length, width = keys.shape
    rows = length // n_feat
    branches = token_ids.shape[0]
    owned = branches // (n_ctx * n_feat)
    padded = -(-GROUP * owned // 16) * 16
    assert n_feat == 2 and length == HEAD

    whole = pl.BlockSpec(memory_space=pltpu.VMEM)
    payload = pl.pallas_call(
        pack_kernel,
        out_shape=jax.ShapeDtypeStruct((length + GATE_ROWS, width), jnp.bfloat16),
        in_specs=[whole] * 3,
        out_specs=whole,
        name="pack",
    )(keys, values, log_gate)
    pairings = swaps(n_ctx)
    order = [1, 0] + list(range(2, len(pairings)))
    near, far = {}, {}
    for step in order:
        near[step] = lax.ppermute(payload, "ctx", pairings[step][0])
    for step in order:
        far[step] = lax.ppermute(near[step], "feat", [(0, 1), (1, 0)])
    steps = range(len(pairings))

    operands = [
        queries, keys, values, log_gate, cand_q, cand_kv.reshape(cand_kv.shape[0], -1),
        token_ids[None], fork_pos[None], slot_map[None],
        *[near[s] for s in steps], *[far[s] for s in steps],
    ]
    return pl.pallas_call(
        functools.partial(main_kernel, n_ctx, n_feat, [pairings[s][1] for s in steps]),
        out_shape=(
            jax.ShapeDtypeStruct((rows, queries.shape[1]), jnp.bfloat16),
            jax.ShapeDtypeStruct((owned, queries.shape[1]), jnp.bfloat16),
        ),
        in_specs=[whole] * len(operands),
        out_specs=(whole, whole),
        scratch_shapes=[
            pltpu.VMEM((GROUP * rows + padded, n_ctx * length), jnp.bfloat16),
            pltpu.VMEM((n_ctx * length, 2 * HEAD), jnp.bfloat16),
            pltpu.VMEM((padded, HEAD), jnp.float32),
        ],
        name="retention",
    )(*operands)


def solution(mesh):
    return jax.shard_map(
        per_device,
        mesh=mesh,
        in_specs=(
            P(("groups", "ctx"), "head"),
            P(("groups", "ctx"), "head"),
            P(("groups", "ctx"), "head"),
            P(("groups", "ctx"), "head"),
            P("groups", "head"),
            P("groups", None, "head"),
            P("groups"),
            P("groups"),
            P("groups"),
        ),
        out_specs=(P(("groups", "ctx", "feat"), "head"), P(("groups", "ctx", "feat"), "head")),
        check_vma=False,
    )
```

time: 863 us -> 28.6 us (0.03); the launches traced: 848 us -> 28.4 us
  waiting for transfers between devices: 362 us -> 12.5 us
  other arithmetic: 171 us -> 0 us
  local copies, waits for them, and re-layouts: 105 us -> 2.75 us
  matrix products: 102 us -> 0 us
  blocking collectives: 82.9 us -> 0 us
  between operations: 25 us -> 0.66 us
    all_gather x1 -> x0, waiting for transfers between devices: 355 us -> none  [carried_in(): everything = jax.tree.map(lambda part: lax.all_gather(part, axis), shard)]
    dot_general x130 -> x0, matrix products: 102 us -> none  [the longest x20 43.4 us: per_device(): lax.dot_general(own_q[:, index * HEAD:(index + 1) * HEAD], key_h, (((1,),...]
    unnamed x1993 -> x16, local copies, waits for them, and re-layouts: 93.3 us -> 2.75 us
    another operation x30 -> x0, other arithmetic: 59.4 us -> none
    all_gather x2 -> x0, blocking collectives: 55.9 us -> none  [carried_in(): everything = jax.tree.map(lambda part: lax.all_gather(part, axis), shard)]
    select_n x9 -> x0, other arithmetic: 39.4 us -> none  [the longest x8 39.4 us: step(): return jax.tree.map(lambda a, b: jnp.where(reached, a, b), new, before)]
    unnamed x1 -> x0, blocking collectives: 26.9 us -> none
    mul x24 -> x0, other arithmetic: 26.6 us -> none  [expand_part(): wide[:, None, :] * partner * weight[None, :, None]]
  transfers between devices with their start and end apart: 4 -> 6, of which waited for: 2 -> 4; matrix products, arithmetic and copies ran while one was open for 24% -> 2% of each run, Pallas kernels for 0% -> 0%
where the time goes in v1:
time: 28.6 us; the launch traced here: 28.4 us
  waiting for transfers between devices  12.5 us (44%)
  Pallas kernels  6.37 us (22%)
  starting transfers between devices  6.15 us (22%)
  local copies, waits for them, and re-layouts  2.75 us (10%)
  between operations  0.66 us (2%)
    ppermute x3, waiting for transfers between devices, per_device(): near[step] = lax.ppermute(payload, 'ctx', pairings[step][0])  12.1 us
    ppermute x3, starting transfers between devices, per_device(): near[step] = lax.ppermute(payload, 'ctx', pairings[step][0])  5.64 us
    pallas_call x1, Pallas kernels, per_device(): pl.pallas_call(functools.partial(main_kernel, n_ctx, n_feat, [pairings[s]...  4.35 us
    unnamed x16, local copies, waits for them, and re-layouts  2.75 us
    pallas_call x1, Pallas kernels, per_device(): pl.pallas_call(pack_kernel, out_shape=jax.ShapeDtypeStruct((length + GATE...  2.02 us
  transfers between devices with their start and end apart: 6, of which 4 were waited for; matrix products, arithmetic and copies ran while one was open for 2% of the time, Pallas kernels for 0%

profile of v1, /device:TPU:0, one launch (start us, length us, event | category | flops | bytes accessed | tf_op | source)
XLA Modules:
  0.0 28.4 jit_solution(5441776399794031812)
XLA Ops:
  0.6 1.4 %copy.12.g_ref.refs_3_ = f32[128,4]{1,0:T(8,128)} copy(f32[128,4]{0,1:T(4,128)} %param.12) | data formatting | bytes 4096 | tf_op args[3]
  2.1 0.0 copy-start.6
  2.1 2.0 %pack.1 = bf16[144,512]{1,0:T(8,128)(2,1)} custom-call(bf16[128,512]{1,0:T(8,128)(2,1)} %refs_1_.1, bf16[128,512]{1,0:T(8,128)(2,1)} %refs_2_.1, f32[128,4]{1,0:T(8,128)} %copy.12.g_ref.refs_3_), custom_call_target="tpu_custom_call" | custom-call | tf_op jit(solution)/shard_map/pack/pallas_call | solution.py:204
  4.1 5.1 %collective-permute-start.2 = (bf16[144,512]{1,0:T(8,128)(2,1)}, bf16[144,512]{1,0:T(8,128)(2,1)S(1)}, u32[]{:S(2)}, u32[]{:S(2)}) collective-permute-start(bf16[144,512]{1,0:T(8,128)(2,1)} %pack.1), channel_id=1, source_target_pairs={{0,12},{4,8},{8,4},{12,0},{1,13},{5,9},{9,5},{13,1},{2,14},{6,10},... | collective-permute-start | bytes 442376 | tf_op jit(solution)/shard_map/ppermute | solution.py:215
  9.2 0.0 collective-permute-start.1
  9.2 0.6 %collective-permute-start = (bf16[144,512]{1,0:T(8,128)(2,1)}, bf16[144,512]{1,0:T(8,128)(2,1)S(1)}, u32[]{:S(2)}, u32[]{:S(2)}) collective-permute-start(bf16[144,512]{1,0:T(8,128)(2,1)} %pack.1), channel_id=1, source_target_pairs={{0,4},{4,0},{8,12},{12,8},{1,5},{5,1},{9,13},{13,9},{2,6},{6,2},{1... | collective-permute-start | bytes 442376 | tf_op jit(solution)/shard_map/ppermute | solution.py:215
  9.7 4.4 %collective-permute-done.2.refs_11_ = bf16[144,512]{1,0:T(8,128)(2,1)S(1)} collective-permute-done((bf16[144,512]{1,0:T(8,128)(2,1)}, bf16[144,512]{1,0:T(8,128)(2,1)S(1)}, u32[]{:S(2)}, u32[]{:S(2)}) %collective-permute-start.2) | collective-permute-done | bytes 147488 | tf_op jit(solution)/shard_map/ppermute | solution.py:215
  14.2 0.0 copy-start
  14.2 0.0 collective-permute-start.5
  14.2 7.7 %collective-permute-done.1.refs_10_ = bf16[144,512]{1,0:T(8,128)(2,1)S(1)} collective-permute-done((bf16[144,512]{1,0:T(8,128)(2,1)}, bf16[144,512]{1,0:T(8,128)(2,1)S(1)}, u32[]{:S(2)}, u32[]{:S(2)}) %collective-permute-start.1) | collective-permute-done | bytes 147488 | tf_op jit(solution)/shard_map/ppermute | solution.py:215
  21.8 0.0 copy-start.1
  21.8 0.0 collective-permute-start.4
  21.8 0.0 collective-permute-done.refs_9_
  21.9 0.0 copy-start.2
  21.9 0.5 %collective-permute-start.3 = (bf16[144,512]{1,0:T(8,128)(2,1)S(1)}, bf16[144,512]{1,0:T(8,128)(2,1)S(1)}, u32[]{:S(2)}, u32[]{:S(2)}) collective-permute-start(bf16[144,512]{1,0:T(8,128)(2,1)S(1)} %collective-permute-done.refs_9_), channel_id=1, source_target_pairs={{0,1},{1,0},{2,3},{3,2},{4,5},{5,4},{6,7},{7,6},{8,9},{9,8},{10,11... | collective-permute-start | bytes 442376 | tf_op jit(solution)/shard_map/ppermute | solution.py:217
  22.4 0.0 copy-done.6
  22.4 0.7 %copy.13 = bf16[8,8,2,512]{3,1,2,0:T(8,128)(2,1)} copy(bf16[8,8,2,512]{3,2,1,0:T(2,128)(2,1)S(1)} %bitcast.6) | data formatting | bytes 262144
  23.0 0.0 collective-permute-done.5.refs_14_
  23.0 0.0 copy-start.3
  23.0 0.2 collective-permute-done.4.refs_13_
  23.2 0.0 copy-start.4
  23.2 0.2 collective-permute-done.3.refs_12_
  23.4 0.0 copy-start.5
  23.4 0.0 copy-done
  23.4 0.0 copy-done.1
  23.4 0.0 copy-done.2
  23.4 0.3 copy-done.3
  23.7 0.2 copy-done.4
  23.9 0.2 copy-done.5
  24.1 4.4 %retention.1 = (bf16[64,2560]{1,0:T(8,128)(2,1)}, bf16[2,2560]{1,0:T(2,128)(2,1)}) custom-call(bf16[128,2560]{1,0:T(8,128)(2,1)} %refs_0_.1, bf16[128,512]{1,0:T(8,128)(2,1)} %refs_1_.1, bf16[128,512]{1,0:T(8,128)(2,1)} %refs_2_.1, f32[128,4]{1,0:T(8,128)} %copy.12.g_ref.refs_3_, bf16[64,2560]{1,0:T(8,128)(2,1)} %refs_4_.1, bf16[64,1024]{1,0:T(8,128)(2,1)} %bitcast.5, ...), custom_call_target="tpu_custom_call" | custom-call | tf_op jit(solution)/shard_map/retention/pallas_call | solution.py:225
Async XLA Ops:
  2.1 20.3 %copy-start.6 = (bf16[64,2,512]{2,1,0:T(2,128)(2,1)S(1)}, bf16[64,2,512]{2,1,0:T(2,128)(2,1)}, u32[]{:S(2)}) copy-start(bf16[64,2,512]{2,1,0:T(2,128)(2,1)} %param.14) | copy-start | bytes 393220
  4.1 10.1 %collective-permute-start.2 = (bf16[144,512]{1,0:T(8,128)(2,1)}, bf16[144,512]{1,0:T(8,128)(2,1)S(1)}, u32[]{:S(2)}, u32[]{:S(2)}) collective-permute-start(bf16[144,512]{1,0:T(8,128)(2,1)} %pack.1), channel_id=1, source_target_pairs={{0,12},{4,8},{8,4},{12,0},{1,13},{5,9},{9,5},{13,1},{2,14},{6,10},... | collective-permute-start | bytes 442376 | tf_op jit(solution)/shard_map/ppermute | solution.py:215
  9.2 12.7 %collective-permute-start.1 = (bf16[144,512]{1,0:T(8,128)(2,1)}, bf16[144,512]{1,0:T(8,128)(2,1)S(1)}, u32[]{:S(2)}, u32[]{:S(2)}) collective-permute-start(bf16[144,512]{1,0:T(8,128)(2,1)} %pack.1), channel_id=1, source_target_pairs={{0,8},{4,12},{8,0},{12,4},{1,9},{5,13},{9,1},{13,5},{2,10},{6,14},... | collective-permute-start | bytes 442376 | tf_op jit(solution)/shard_map/ppermute | solution.py:215
  9.2 12.7 %collective-permute-start = (bf16[144,512]{1,0:T(8,128)(2,1)}, bf16[144,512]{1,0:T(8,128)(2,1)S(1)}, u32[]{:S(2)}, u32[]{:S(2)}) collective-permute-start(bf16[144,512]{1,0:T(8,128)(2,1)} %pack.1), channel_id=1, source_target_pairs={{0,4},{4,0},{8,12},{12,8},{1,5},{5,1},{9,13},{13,9},{2,6},{6,2},{1... | collective-permute-start | bytes 442376 | tf_op jit(solution)/shard_map/ppermute | solution.py:215
  14.2 9.3 %copy-start = (bf16[144,512]{1,0:T(8,128)(2,1)}, bf16[144,512]{1,0:T(8,128)(2,1)S(1)}, u32[]{:S(2)}) copy-start(bf16[144,512]{1,0:T(8,128)(2,1)S(1)} %collective-permute-done.2.refs_11_) | copy-start | bytes 442372
  14.2 8.9 %collective-permute-start.5 = (bf16[144,512]{1,0:T(8,128)(2,1)S(1)}, bf16[144,512]{1,0:T(8,128)(2,1)S(1)}, u32[]{:S(2)}, u32[]{:S(2)}) collective-permute-start(bf16[144,512]{1,0:T(8,128)(2,1)S(1)} %collective-permute-done.2.refs_11_), channel_id=1, source_target_pairs={{0,1},{1,0},{2,3},{3,2},{4,5},{5,4},{6,7},{7,6},{8,9},{9,8},{10,11... | collective-permute-start | bytes 442376 | tf_op jit(solution)/shard_map/ppermute | solution.py:217
  21.8 1.6 %copy-start.1 = (bf16[144,512]{1,0:T(8,128)(2,1)}, bf16[144,512]{1,0:T(8,128)(2,1)S(1)}, u32[]{:S(2)}) copy-start(bf16[144,512]{1,0:T(8,128)(2,1)S(1)} %collective-permute-done.1.refs_10_) | copy-start | bytes 442372
  21.8 1.4 %collective-permute-start.4 = (bf16[144,512]{1,0:T(8,128)(2,1)S(1)}, bf16[144,512]{1,0:T(8,128)(2,1)S(1)}, u32[]{:S(2)}, u32[]{:S(2)}) collective-permute-start(bf16[144,512]{1,0:T(8,128)(2,1)S(1)} %collective-permute-done.1.refs_10_), channel_id=1, source_target_pairs={{0,1},{1,0},{2,3},{3,2},{4,5},{5,4},{6,7},{7,6},{8,9},{9,8},{10,11... | collective-permute-start | bytes 442376 | tf_op jit(solution)/shard_map/ppermute | solution.py:217
  21.9 1.6 %copy-start.2 = (bf16[144,512]{1,0:T(8,128)(2,1)}, bf16[144,512]{1,0:T(8,128)(2,1)S(1)}, u32[]{:S(2)}) copy-start(bf16[144,512]{1,0:T(8,128)(2,1)S(1)} %collective-permute-done.refs_9_) | copy-start | bytes 442372
  21.9 1.6 %collective-permute-start.3 = (bf16[144,512]{1,0:T(8,128)(2,1)S(1)}, bf16[144,512]{1,0:T(8,128)(2,1)S(1)}, u32[]{:S(2)}, u32[]{:S(2)}) collective-permute-start(bf16[144,512]{1,0:T(8,128)(2,1)S(1)} %collective-permute-done.refs_9_), channel_id=1, source_target_pairs={{0,1},{1,0},{2,3},{3,2},{4,5},{5,4},{6,7},{7,6},{8,9},{9,8},{10,11... | collective-permute-start | bytes 442376 | tf_op jit(solution)/shard_map/ppermute | solution.py:217
  23.0 0.7 %copy-start.3 = (bf16[144,512]{1,0:T(8,128)(2,1)}, bf16[144,512]{1,0:T(8,128)(2,1)S(1)}, u32[]{:S(2)}) copy-start(bf16[144,512]{1,0:T(8,128)(2,1)S(1)} %collective-permute-done.5.refs_14_) | copy-start | bytes 442372
  23.2 0.7 %copy-start.4 = (bf16[144,512]{1,0:T(8,128)(2,1)}, bf16[144,512]{1,0:T(8,128)(2,1)S(1)}, u32[]{:S(2)}) copy-start(bf16[144,512]{1,0:T(8,128)(2,1)S(1)} %collective-permute-done.4.refs_13_) | copy-start | bytes 442372
  23.4 0.7 %copy-start.5 = (bf16[144,512]{1,0:T(8,128)(2,1)}, bf16[144,512]{1,0:T(8,128)(2,1)S(1)}, u32[]{:S(2)}) copy-start(bf16[144,512]{1,0:T(8,128)(2,1)S(1)} %collective-permute-done.3.refs_12_) | copy-start | bytes 442372

commit v2 on v1

v2 whole, which is shorter than its diff:
```python
import functools

import jax
import jax.numpy as jnp
from jax import lax
from jax.experimental import pallas as pl
from jax.experimental.pallas import tpu as pltpu
from jax.sharding import PartitionSpec as P


HEAD = 128
GROUP = 5
GATE_ROWS = 8
MASKED = -1e30
SCALE = 1.0 / HEAD


def dot(a, b, contract, precision=None):
    return lax.dot_general(
        a, b, ((contract[:1], contract[1:]), ((), ())),
        precision=precision, preferred_element_type=jnp.float32,
    )


def exact_dot(a, b, contract):
    return dot(a, b, contract, lax.Precision.HIGHEST)


def gate_sums(gate):
    length = gate.shape[1]
    row = lax.broadcasted_iota(jnp.int32, (length, length), 0)
    col = lax.broadcasted_iota(jnp.int32, (length, length), 1)
    after = exact_dot(gate, (row > col).astype(jnp.float32), (1, 0))
    upto = exact_dot(gate, (row <= col).astype(jnp.float32), (1, 0))
    return after, upto


def split3(x):
    high = x.astype(jnp.bfloat16)
    rest = x - high.astype(jnp.float32)
    middle = rest.astype(jnp.bfloat16)
    low = (rest - middle.astype(jnp.float32)).astype(jnp.bfloat16)
    return [part.astype(jnp.float32) for part in (high, middle, low)]


def pack_kernel(k_ref, v_ref, g_ref, out_ref, gate_ref, sem):
    length, width = k_ref.shape
    body = out_ref.at[pl.ds(0, length), :]
    from_k = pltpu.make_async_copy(k_ref, body, sem.at[0])
    from_v = pltpu.make_async_copy(v_ref, body, sem.at[0])
    gates = pltpu.make_async_copy(g_ref, gate_ref, sem.at[1])
    first_core = lax.axis_index("feat") == 0
    gates.start()
    pl.when(first_core)(from_k.start)
    pl.when(jnp.logical_not(first_core))(from_v.start)
    gates.wait()
    after, upto = gate_sums(gate_ref[...])
    place = lax.broadcasted_iota(jnp.int32, (GATE_ROWS, length), 0)
    for head in range(width // HEAD):
        total = jnp.broadcast_to(upto[head : head + 1, length - 1 :], (1, length))
        parts = split3(after[head : head + 1, :]) + split3(total)
        tile = jnp.zeros((GATE_ROWS, length), jnp.float32)
        for i, part in enumerate(parts):
            tile = jnp.where(place == i, part, tile)
        out_ref[length:, head * HEAD : (head + 1) * HEAD] = tile.astype(jnp.bfloat16)
    pl.when(first_core)(from_k.wait)
    pl.when(jnp.logical_not(first_core))(from_v.wait)


def own_kernel(n_feat, *refs):
    sources, outs, bufs, sem = refs[:9], refs[9:15], refs[15:24], refs[24]
    queries_acc = outs
    qa_ref, acc_ref, own_ref, row_ref, fork_out, gate_out = queries_acc
    q_ref, k_ref, v_ref, g_ref, cq_ref, ckv_ref, tok_ref, fork_ref, slot_ref = bufs

    ctx = lax.axis_index("ctx")
    feat = lax.axis_index("feat")
    rows = q_ref.shape[0]
    length, width = k_ref.shape
    heads = width // HEAD
    padded = qa_ref.shape[1] - GROUP * rows
    start = pl.multiple_of(feat * rows, rows)
    copies = []
    for i, (source, buf) in enumerate(zip(sources, bufs)):
        origin = source.at[pl.ds(start, rows), :] if i == 0 else source
        copies.append(pltpu.make_async_copy(origin, buf, sem.at[i]))
    for copy in copies:
        copy.start()
    for copy in copies:
        copy.wait()

    gate = g_ref[...]
    after, upto = gate_sums(gate)
    gate_out[:heads, :] = after
    gate_out[heads:, :] = jnp.broadcast_to(upto[:, length - 1 :], (heads, length))
    row = lax.broadcasted_iota(jnp.int32, (rows, length), 0) + start
    col = lax.broadcasted_iota(jnp.int32, (rows, length), 1)
    causal = col <= row
    row_sum = exact_dot(causal.astype(jnp.float32), gate, (1, 1))
    row_ref[...] = row_sum

    owned = tok_ref.shape[1] // (lax.axis_size("ctx") * n_feat)
    line = lax.broadcasted_iota(jnp.int32, (padded, 1), 0)
    slot = (ctx * n_feat + feat) * owned + lax.rem(line, owned)
    mine = slot_ref[...] == slot
    pick_id = jnp.sum(jnp.where(mine, tok_ref[...].astype(jnp.float32), 0.0), axis=1, keepdims=True)
    fork = jnp.sum(jnp.where(mine, fork_ref[...].astype(jnp.float32), 0.0), axis=1, keepdims=True)
    fork_out[...] = jnp.broadcast_to(fork.astype(jnp.int32), fork_out.shape)
    cands = cq_ref.shape[0]
    pick = (
        lax.broadcasted_iota(jnp.int32, (padded, cands), 1).astype(jnp.float32) == pick_id
    ).astype(jnp.bfloat16)

    ones = jnp.ones((length, HEAD), jnp.bfloat16)
    for head in range(heads):
        lanes = slice(head * HEAD, (head + 1) * HEAD)
        picked = dot(pick, cq_ref[:, head * GROUP * HEAD : (head + 1) * GROUP * HEAD], (1, 0))
        branch_q = jnp.zeros((padded, HEAD), jnp.float32)
        for member in range(GROUP):
            chosen = (line >= member * owned) & (line < (member + 1) * owned)
            branch_q = jnp.where(chosen, picked[:, member * HEAD : (member + 1) * HEAD], branch_q)
        for member in range(GROUP):
            column = (head * GROUP + member) * HEAD
            qa_ref[head, member * rows : (member + 1) * rows, :] = q_ref[:, column : column + HEAD]
        qa_ref[head, GROUP * rows :, :] = branch_q.astype(jnp.bfloat16)

        reach = jnp.where(causal, row_sum[:, head : head + 1] - upto[head : head + 1, :], MASKED)
        decay = jnp.exp(reach) * SCALE
        branch_decay = jnp.exp(after[head : head + 1, :]) * SCALE
        raw = dot(qa_ref[head], k_ref[:, lanes], (1, 1))
        square = raw * raw
        weights = [
            (square[m * rows : (m + 1) * rows] * decay).astype(jnp.bfloat16) for m in range(GROUP)
        ]
        weights.append((square[GROUP * rows :] * branch_decay).astype(jnp.bfloat16))
        value = jnp.concatenate([v_ref[:, lanes], ones], axis=1)
        acc_ref[head] = dot(jnp.concatenate(weights, axis=0), value, (1, 0))

        new_k = dot(pick, ckv_ref[:, 0, lanes], (1, 0))
        new_v = dot(pick, ckv_ref[:, 1, lanes], (1, 0))
        inner = jnp.sum(branch_q * new_k, axis=1, keepdims=True)
        weight = inner * inner * SCALE
        own_ref[head, :, :HEAD] = weight * new_v
        own_ref[head, :, HEAD:] = jnp.broadcast_to(weight, (padded, HEAD))


def rest_kernel(partners, *refs):
    count = len(partners)
    qa_ref, acc_ref, own_ref, row_ref, fork_ref, gate_ref = refs[:6]
    near, far = refs[6 : 6 + count], refs[6 + count : 6 + 2 * count]
    out_ref, branch_ref, w_ref, value_ref, key_ref, line_ref = refs[6 + 2 * count :]

    ctx = lax.axis_index("ctx")
    first_core = lax.axis_index("feat") == 0
    rows = out_ref.shape[0]
    owned = branch_ref.shape[0]
    heads, total_rows, _ = qa_ref.shape
    padded = total_rows - GROUP * rows
    length = gate_ref.shape[1]
    others = [partner(ctx) for partner in partners]
    fork = fork_ref[...]
    value_ref[:, HEAD:] = jnp.ones((value_ref.shape[0], HEAD), jnp.bfloat16)
    for head in range(heads):
        lanes = slice(head * HEAD, (head + 1) * HEAD)
        row_h = row_ref[:, head : head + 1]
        tails, totals = [], []
        for i in range(count):
            part = near[i][length:, lanes].astype(jnp.float32)
            tails.append(part[0:1] + part[1:2] + part[2:3])
            totals.append(part[3:4] + part[4:5] + part[5:6])
            here, there = near[i][:length, lanes], far[i][:length, lanes]
            key_ref[i * length : (i + 1) * length, :] = jnp.where(first_core, here, there)
            value_ref[i * length : (i + 1) * length, :HEAD] = jnp.where(first_core, there, here)
        raw = dot(qa_ref[head], key_ref[...], (1, 1))
        square = raw * raw
        between_own = jnp.zeros((padded, length), jnp.float32)
        for b, block in enumerate(others):
            between_own = between_own + jnp.where((block > ctx) & (block < fork), totals[b], 0.0)
            between = tails[b]
            past = tails[b] + jnp.where(
                (ctx > block) & (ctx < fork), gate_ref[heads + head : heads + head + 1, :], 0.0
            )
            for o, other in enumerate(others):
                if o != b:
                    between = between + jnp.where((other > block) & (other < ctx), totals[o], 0.0)
                    past = past + jnp.where((other > block) & (other < fork), totals[o], 0.0)
            decay = jnp.exp(jnp.where(block < ctx, row_h + between, MASKED)) * SCALE
            branch_decay = jnp.exp(jnp.where(block < fork, past, MASKED)) * SCALE
            cols = slice(b * length, (b + 1) * length)
            for member in range(GROUP):
                span = slice(member * rows, (member + 1) * rows)
                w_ref[span, cols] = (square[span, cols] * decay).astype(jnp.bfloat16)
            w_ref[GROUP * rows :, cols] = (square[GROUP * rows :, cols] * branch_decay).astype(
                jnp.bfloat16
            )
        total = dot(w_ref[...], value_ref[...], (1, 0))
        prefill = total[: GROUP * rows] + acc_ref[head, : GROUP * rows, :]
        ratio = prefill[:, :HEAD] / jnp.maximum(prefill[:, HEAD:], 1.0)
        for member in range(GROUP):
            column = (head * GROUP + member) * HEAD
            out_ref[:, column : column + HEAD] = ratio[member * rows : (member + 1) * rows].astype(
                out_ref.dtype
            )
        kept = jnp.exp(jnp.where(ctx < fork, between_own, MASKED))
        branch = total[GROUP * rows :] + own_ref[head]
        before = acc_ref[head, GROUP * rows :, :]
        numer = branch[:, :HEAD] + kept * before[:, :HEAD]
        denom = branch[:, HEAD:] + kept * before[:, HEAD:]
        line_ref[...] = numer / jnp.maximum(denom, 1.0)
        for member in range(GROUP):
            column = (head * GROUP + member) * HEAD
            branch_ref[:, column : column + HEAD] = line_ref[
                member * owned : (member + 1) * owned, :
            ].astype(branch_ref.dtype)


def swaps(count):
    if count & (count - 1) == 0:
        return [
            ([(i, i ^ step) for i in range(count)], functools.partial(lambda s, i: i ^ s, step))
            for step in range(1, count)
        ]
    return [
        (
            [(i, (i + step) % count) for i in range(count)],
            functools.partial(lambda s, i: lax.rem(i + count - s, count), step),
        )
        for step in range(1, count)
    ]


ORDER = (2, 1, 3)


def per_device(queries, keys, values, log_gate, cand_q, cand_kv, token_ids, fork_pos, slot_map):
    n_ctx = lax.axis_size("ctx")
    n_feat = lax.axis_size("feat")
    length, width = keys.shape
    heads = width // HEAD
    rows = length // n_feat
    branches = token_ids.shape[0]
    owned = branches // (n_ctx * n_feat)
    padded = -(-GROUP * owned // 16) * 16
    total_rows = GROUP * rows + padded
    assert n_feat == 2 and length == HEAD

    hbm = pl.BlockSpec(memory_space=pltpu.HBM)
    vmem = pl.BlockSpec(memory_space=pltpu.VMEM)
    in_hbm = lambda x: pltpu.with_memory_space_constraint(x, pltpu.HBM)
    gates = in_hbm(log_gate.T)
    payload = pl.pallas_call(
        pack_kernel,
        out_shape=jax.ShapeDtypeStruct((length + GATE_ROWS, width), jnp.bfloat16),
        in_specs=[hbm] * 3,
        out_specs=vmem,
        scratch_shapes=[
            pltpu.VMEM(gates.shape, gates.dtype),
            pltpu.SemaphoreType.DMA((2,)),
        ],
        compiler_params=pltpu.CompilerParams(vmem_limit_bytes=4 << 20),
        name="pack",
    )(in_hbm(keys), in_hbm(values), gates)
    pairings = swaps(n_ctx)
    count = len(pairings)
    steps = [s - 1 for s in ORDER] if count == 3 else list(range(count))
    near, far = [], []
    for s in steps:
        near.append(lax.ppermute(payload, "ctx", pairings[s][0]))
    for part in near:
        far.append(lax.ppermute(part, "feat", [(0, 1), (1, 0)]))
    partners = [pairings[s][1] for s in steps]

    sources = [
        queries, keys, values, gates, cand_q, cand_kv,
        token_ids[None], fork_pos[None], slot_map[None],
    ]
    own = pl.pallas_call(
        functools.partial(own_kernel, n_feat),
        out_shape=(
            jax.ShapeDtypeStruct((heads, total_rows, HEAD), jnp.bfloat16),
            jax.ShapeDtypeStruct((heads, total_rows, 2 * HEAD), jnp.float32),
            jax.ShapeDtypeStruct((heads, padded, 2 * HEAD), jnp.float32),
            jax.ShapeDtypeStruct((rows, heads), jnp.float32),
            jax.ShapeDtypeStruct((padded, length), jnp.int32),
            jax.ShapeDtypeStruct((2 * heads, length), jnp.float32),
        ),
        in_specs=[hbm] * len(sources),
        out_specs=(vmem,) * 6,
        scratch_shapes=[pltpu.VMEM((rows, queries.shape[1]), queries.dtype)]
        + [pltpu.VMEM(s.shape, s.dtype) for s in sources[1:]]
        + [pltpu.SemaphoreType.DMA((len(sources),))],
        compiler_params=pltpu.CompilerParams(vmem_limit_bytes=16 << 20),
        cost_estimate=pl.CostEstimate(flops=1 << 30, bytes_accessed=8 << 20, transcendentals=0),
        name="own",
    )(*[in_hbm(s) for s in sources])
    operands = [*own, *near, *far]
    return pl.pallas_call(
        functools.partial(rest_kernel, partners),
        out_shape=(
            jax.ShapeDtypeStruct((rows, queries.shape[1]), jnp.bfloat16),
            jax.ShapeDtypeStruct((owned, queries.shape[1]), jnp.bfloat16),
        ),
        in_specs=[vmem] * len(operands),
        out_specs=(vmem, vmem),
        scratch_shapes=[
            pltpu.VMEM((total_rows, count * length), jnp.bfloat16),
            pltpu.VMEM((count * length, 2 * HEAD), jnp.bfloat16),
            pltpu.VMEM((count * length, HEAD), jnp.bfloat16),
            pltpu.VMEM((padded, HEAD), jnp.float32),
        ],
        compiler_params=pltpu.CompilerParams(vmem_limit_bytes=16 << 20),
        name="rest",
    )(*operands)


def solution(mesh):
    return sharded(mesh)


def sharded(mesh):
    return jax.shard_map(
        per_device,
        mesh=mesh,
        in_specs=(
            P(("groups", "ctx"), "head"),
            P(("groups", "ctx"), "head"),
            P(("groups", "ctx"), "head"),
            P(("groups", "ctx"), "head"),
            P("groups", "head"),
            P("groups", None, "head"),
            P("groups"),
            P("groups"),
            P("groups"),
        ),
        out_specs=(P(("groups", "ctx", "feat"), "head"), P(("groups", "ctx", "feat"), "head")),
        check_vma=False,
    )
```

time: 28.6 us -> 23.6 us (0.83)
  local copies, waits for them, and re-layouts: 2.75 us -> 0 us
  waiting for transfers between devices: 12.5 us -> 11.1 us
  Pallas kernels: 6.37 us -> 5.82 us
  starting transfers between devices: 6.15 us -> 5.79 us
    unnamed x16 -> x0, local copies, waits for them, and re-layouts: 2.75 us -> none
    ppermute x6, waiting for transfers between devices: 12.5 us -> 11.1 us  [the longest x3 11.1 us: per_device(): near.append(lax.ppermute(payload, 'ctx', pairings[s][0]))]
    pallas_call x1, Pallas kernels: 2.02 us -> 1 us  [per_device(): pl.pallas_call(pack_kernel, out_shape=jax.ShapeDtypeStruct((length + GATE...]
    pallas_call x1 -> x2, Pallas kernels: 4.35 us -> 4.82 us  [the longest x1 2.77 us: per_device(): pl.pallas_call(functools.partial(own_kernel, n_feat), out_shape=(jax.Shap...]
    ppermute x6, starting transfers between devices: 6.15 us -> 5.79 us  [the longest x3 5.78 us: per_device(): near.append(lax.ppermute(payload, 'ctx', pairings[s][0]))]
  transfers between devices with their start and end apart: 6 -> 6, of which waited for: 4 -> 3; matrix products, arithmetic and copies ran while one was open for 2% -> 0% of each run, Pallas kernels for 0% -> 12%
where the time goes in v2:
time: 23.6 us; the launch traced here: 23.4 us
  waiting for transfers between devices  11.1 us (47%)
  Pallas kernels  5.82 us (25%)
  starting transfers between devices  5.79 us (25%)
  between operations  0.67 us (3%)
    ppermute x3, waiting for transfers between devices, per_device(): near.append(lax.ppermute(payload, 'ctx', pairings[s][0]))  11.1 us
    ppermute x3, starting transfers between devices, per_device(): near.append(lax.ppermute(payload, 'ctx', pairings[s][0]))  5.78 us
    pallas_call x1, Pallas kernels, per_device(): pl.pallas_call(functools.partial(own_kernel, n_feat), out_shape=(jax.Shap...  2.77 us
    pallas_call x1, Pallas kernels, per_device(): pl.pallas_call(functools.partial(rest_kernel, partners), out_shape=(jax.S...  2.04 us
    pallas_call x1, Pallas kernels, per_device(): pl.pallas_call(pack_kernel, out_shape=jax.ShapeDtypeStruct((length + GATE...  1 us
  transfers between devices with their start and end apart: 6, of which 3 were waited for; matrix products, arithmetic and copies ran while one was open for 0% of the time, Pallas kernels for 12%

profile of v2, /device:TPU:0, one launch (start us, length us, event | category | flops | bytes accessed | tf_op | source)
XLA Modules:
  0.0 23.4 jit_solution(16444277307200386900)
XLA Ops:
  0.6 1.0 %pack.1 = bf16[136,512]{1,0:T(8,128)(2,1)S(1)} custom-call(bf16[128,512]{1,0:T(8,128)(2,1)} %k_ref.1, bf16[128,512]{1,0:T(8,128)(2,1)} %v_ref.1, f32[4,128]{1,0:T(4,128)} %bitcast.4), custom_call_target="tpu_custom_call" | custom-call | tf_op jit(solution)/shard_map/pack/pallas_call | solution.py:251
  1.6 5.1 %collective-permute-start.2 = (bf16[136,512]{1,0:T(8,128)(2,1)S(1)}, bf16[136,512]{1,0:T(8,128)(2,1)S(1)}, u32[]{:S(2)}, u32[]{:S(2)}) collective-permute-start(bf16[136,512]{1,0:T(8,128)(2,1)S(1)} %pack.1), channel_id=1, source_target_pairs={{0,12},{4,8},{8,4},{12,0},{1,13},{5,9},{9,5},{13,1},{2,14},{6,10},... | collective-permute-start | bytes 417800 | tf_op jit(solution)/shard_map/ppermute | solution.py:268
  6.8 0.0 collective-permute-start.1
  6.8 0.6 %collective-permute-start = (bf16[136,512]{1,0:T(8,128)(2,1)S(1)}, bf16[136,512]{1,0:T(8,128)(2,1)S(1)}, u32[]{:S(2)}, u32[]{:S(2)}) collective-permute-start(bf16[136,512]{1,0:T(8,128)(2,1)S(1)} %pack.1), channel_id=1, source_target_pairs={{0,8},{4,12},{8,0},{12,4},{1,9},{5,13},{9,1},{13,5},{2,10},{6,14},... | collective-permute-start | bytes 417800 | tf_op jit(solution)/shard_map/ppermute | solution.py:268
  7.4 3.9 %collective-permute-done.2.refs_8_ = bf16[136,512]{1,0:T(8,128)(2,1)S(1)} collective-permute-done((bf16[136,512]{1,0:T(8,128)(2,1)S(1)}, bf16[136,512]{1,0:T(8,128)(2,1)S(1)}, u32[]{:S(2)}, u32[]{:S(2)}) %collective-permute-start.2) | collective-permute-done | bytes 139296 | tf_op jit(solution)/shard_map/ppermute | solution.py:268
  11.4 0.0 collective-permute-start.5
  11.4 3.2 %collective-permute-done.1.refs_7_ = bf16[136,512]{1,0:T(8,128)(2,1)S(1)} collective-permute-done((bf16[136,512]{1,0:T(8,128)(2,1)S(1)}, bf16[136,512]{1,0:T(8,128)(2,1)S(1)}, u32[]{:S(2)}, u32[]{:S(2)}) %collective-permute-start.1) | collective-permute-done | bytes 139296 | tf_op jit(solution)/shard_map/ppermute | solution.py:268
  14.5 0.0 collective-permute-start.4
  14.5 4.0 %collective-permute-done.refs_6_ = bf16[136,512]{1,0:T(8,128)(2,1)S(1)} collective-permute-done((bf16[136,512]{1,0:T(8,128)(2,1)S(1)}, bf16[136,512]{1,0:T(8,128)(2,1)S(1)}, u32[]{:S(2)}, u32[]{:S(2)}) %collective-permute-start) | collective-permute-done | bytes 139296 | tf_op jit(solution)/shard_map/ppermute | solution.py:268
  18.6 0.0 collective-permute-start.3
  18.6 2.8 %own.1 = (bf16[4,336,128]{2,1,0:T(8,128)(2,1)S(1)}, f32[4,336,256]{2,1,0:T(8,128)S(1)}, f32[4,16,256]{2,1,0:T(8,128)S(1)}, f32[64,4]{1,0:T(8,128)S(1)}, s32[16,128]{1,0:T(8,128)S(1)}, /*index=5*/f32[8,128]{1,0:T(8,128)S(1)}) custom-call(bf16[128,2560]{1,0:T(8,128)(2,1)} %refs_0_.1, bf16[128,512]{1,0:T(8,128)(2,1)} %k_ref.1, bf16[128,512]{1,0:T(8,128)(2,1)} %v_ref.1, ...), custom_call_target="tpu_custom_call" | custom-call | flops 1073741824 | bytes 8388608 | tf_op jit(solution)/shard_map/own/pallas_call | solution.py:277
  21.3 0.0 collective-permute-done.5.refs_11_
  21.4 0.0 collective-permute-done.4.refs_10_
  21.4 0.0 collective-permute-done.3.refs_9_
  21.4 2.0 %rest.1 = (bf16[64,2560]{1,0:T(8,128)(2,1)}, bf16[2,2560]{1,0:T(2,128)(2,1)}) custom-call(bf16[4,336,128]{2,1,0:T(8,128)(2,1)S(1)} %get-tuple-element.8.refs_0_, f32[4,336,256]{2,1,0:T(8,128)S(1)} %get-tuple-element.9.refs_1_, f32[4,16,256]{2,1,0:T(8,128)S(1)} %get-tuple-element.10.refs_2_, f32[64,4]{1,0:T(8,128)S(1)} %get-tuple-element.11.refs_3_, ...), custom_call_target="tpu_custom_call" | custom-call | tf_op jit(solution)/shard_map/rest/pallas_call | solution.py:297
Async XLA Ops:
  1.6 9.7 %collective-permute-start.2 = (bf16[136,512]{1,0:T(8,128)(2,1)S(1)}, bf16[136,512]{1,0:T(8,128)(2,1)S(1)}, u32[]{:S(2)}, u32[]{:S(2)}) collective-permute-start(bf16[136,512]{1,0:T(8,128)(2,1)S(1)} %pack.1), channel_id=1, source_target_pairs={{0,12},{4,8},{8,4},{12,0},{1,13},{5,9},{9,5},{13,1},{2,14},{6,10},... | collective-permute-start | bytes 417800 | tf_op jit(solution)/shard_map/ppermute | solution.py:268
  6.8 7.7 %collective-permute-start.1 = (bf16[136,512]{1,0:T(8,128)(2,1)S(1)}, bf16[136,512]{1,0:T(8,128)(2,1)S(1)}, u32[]{:S(2)}, u32[]{:S(2)}) collective-permute-start(bf16[136,512]{1,0:T(8,128)(2,1)S(1)} %pack.1), channel_id=1, source_target_pairs={{0,4},{4,0},{8,12},{12,8},{1,5},{5,1},{9,13},{13,9},{2,6},{6,2},{1... | collective-permute-start | bytes 417800 | tf_op jit(solution)/shard_map/ppermute | solution.py:268
  6.8 11.8 %collective-permute-start = (bf16[136,512]{1,0:T(8,128)(2,1)S(1)}, bf16[136,512]{1,0:T(8,128)(2,1)S(1)}, u32[]{:S(2)}, u32[]{:S(2)}) collective-permute-start(bf16[136,512]{1,0:T(8,128)(2,1)S(1)} %pack.1), channel_id=1, source_target_pairs={{0,8},{4,12},{8,0},{12,4},{1,9},{5,13},{9,1},{13,5},{2,10},{6,14},... | collective-permute-start | bytes 417800 | tf_op jit(solution)/shard_map/ppermute | solution.py:268
  11.4 10.0 %collective-permute-start.5 = (bf16[136,512]{1,0:T(8,128)(2,1)S(1)}, bf16[136,512]{1,0:T(8,128)(2,1)S(1)}, u32[]{:S(2)}, u32[]{:S(2)}) collective-permute-start(bf16[136,512]{1,0:T(8,128)(2,1)S(1)} %collective-permute-done.2.refs_8_), channel_id=1, source_target_pairs={{0,1},{1,0},{2,3},{3,2},{4,5},{5,4},{6,7},{7,6},{8,9},{9,8},{10,11... | collective-permute-start | bytes 417800 | tf_op jit(solution)/shard_map/ppermute | solution.py:270
  14.5 6.8 %collective-permute-start.4 = (bf16[136,512]{1,0:T(8,128)(2,1)S(1)}, bf16[136,512]{1,0:T(8,128)(2,1)S(1)}, u32[]{:S(2)}, u32[]{:S(2)}) collective-permute-start(bf16[136,512]{1,0:T(8,128)(2,1)S(1)} %collective-permute-done.1.refs_7_), channel_id=1, source_target_pairs={{0,1},{1,0},{2,3},{3,2},{4,5},{5,4},{6,7},{7,6},{8,9},{9,8},{10,11... | collective-permute-start | bytes 417800 | tf_op jit(solution)/shard_map/ppermute | solution.py:270
  18.6 2.8 %collective-permute-start.3 = (bf16[136,512]{1,0:T(8,128)(2,1)S(1)}, bf16[136,512]{1,0:T(8,128)(2,1)S(1)}, u32[]{:S(2)}, u32[]{:S(2)}) collective-permute-start(bf16[136,512]{1,0:T(8,128)(2,1)S(1)} %collective-permute-done.refs_6_), channel_id=1, source_target_pairs={{0,1},{1,0},{2,3},{3,2},{4,5},{5,4},{6,7},{7,6},{8,9},{9,8},{10,11... | collective-permute-start | bytes 417800 | tf_op jit(solution)/shard_map/ppermute | solution.py:270

commit v3 on v2

v3 whole, which is shorter than its diff:
```python
import functools

import jax
import jax.numpy as jnp
from jax import lax
from jax.experimental import pallas as pl
from jax.experimental.pallas import tpu as pltpu
from jax.sharding import PartitionSpec as P


HEAD = 128
GROUP = 5
MASKED = -1e30
SCALE = 1.0 / HEAD


def dot(a, b, contract, precision=None):
    return lax.dot_general(
        a, b, ((contract[:1], contract[1:]), ((), ())),
        precision=precision, preferred_element_type=jnp.float32,
    )


def exact_dot(a, b, contract):
    return dot(a, b, contract, lax.Precision.HIGHEST)


def triangle(length, keep):
    row = lax.broadcasted_iota(jnp.int32, (length, length), 0)
    col = lax.broadcasted_iota(jnp.int32, (length, length), 1)
    return keep(row, col).astype(jnp.float32)


def from_inclusive(inclusive):
    lane = lax.broadcasted_iota(jnp.int32, inclusive.shape, 1)
    last = inclusive.shape[1] - 1
    after = jnp.where(lane == last, 0.0, pltpu.roll(inclusive, last, 1))
    total = jnp.broadcast_to(inclusive[:, :1], inclusive.shape)
    return after, total


def received_gates(ref, heads, first_core):
    tile = ref[ref.shape[0] - gate_rows(heads) :, :].astype(jnp.float32)
    mixed = tile + pltpu.roll(tile, tile.shape[0] - heads, 0)
    after, total = from_inclusive(mixed)
    after = jnp.where(first_core, after, pltpu.roll(after, after.shape[1] // 2, 1))
    return after, total


def gate_rows(heads):
    return -(-2 * heads // 8) * 8


def pack_kernel(k_ref, v_ref, g_ref, out_ref, gate_ref, sem):
    length, width = k_ref.shape
    heads = width // HEAD
    half = length // 2
    start = pl.multiple_of(lax.axis_index("feat") * half, half)
    gates = pltpu.make_async_copy(g_ref, gate_ref, sem.at[0])
    gates.start()
    copies = []
    for i, ref in enumerate((k_ref, v_ref)):
        for head in range(heads):
            copies.append(
                pltpu.make_async_copy(
                    ref.at[pl.ds(start, half), pl.ds(head * HEAD, HEAD)],
                    out_ref.at[pl.ds((i * heads + head) * half, half), :],
                    sem.at[1 + i * heads + head],
                )
            )
    for copy in copies:
        copy.start()
    gates.wait()
    inclusive = exact_dot(gate_ref[...], triangle(length, lambda r, c: r >= c), (1, 0))
    high = inclusive.astype(jnp.bfloat16).astype(jnp.float32)
    parts = [high, inclusive - high]
    spare = gate_rows(heads) - 2 * heads
    if spare:
        parts.append(jnp.zeros((spare, length), jnp.float32))
    out_ref[2 * heads * half :, :] = jnp.concatenate(parts, axis=0).astype(jnp.bfloat16)
    for copy in copies:
        copy.wait()


def own_kernel(n_feat, *refs):
    sources, outs, bufs, sem = refs[:9], refs[9:15], refs[15:24], refs[24]
    qa_ref, acc_ref, own_ref, row_ref, fork_out, gate_out = outs
    q_ref, k_ref, v_ref, g_ref, cq_ref, ckv_ref, tok_ref, fork_ref, slot_ref = bufs

    ctx = lax.axis_index("ctx")
    feat = lax.axis_index("feat")
    rows = q_ref.shape[0]
    length, width = k_ref.shape
    heads = width // HEAD
    padded = qa_ref.shape[1] - GROUP * rows
    start = pl.multiple_of(feat * rows, rows)
    copies = []
    for i, (source, buf) in enumerate(zip(sources, bufs)):
        origin = source.at[pl.ds(start, rows), :] if i == 0 else source
        copies.append(pltpu.make_async_copy(origin, buf, sem.at[i]))
    for copy in copies:
        copy.start()
    for copy in copies:
        copy.wait()

    gate = g_ref[...]
    upto = exact_dot(gate, triangle(length, lambda r, c: r <= c), (1, 0))
    after = exact_dot(gate, triangle(length, lambda r, c: r > c), (1, 0))
    gate_out[...] = jnp.broadcast_to(upto[:, length - 1 :], (heads, length))
    row = lax.broadcasted_iota(jnp.int32, (rows, length), 0) + start
    col = lax.broadcasted_iota(jnp.int32, (rows, length), 1)
    causal = col <= row
    row_sum = exact_dot(causal.astype(jnp.float32), gate, (1, 1))
    row_ref[...] = row_sum

    owned = tok_ref.shape[1] // (lax.axis_size("ctx") * n_feat)
    line = lax.broadcasted_iota(jnp.int32, (padded, 1), 0)
    slot = (ctx * n_feat + feat) * owned + lax.rem(line, owned)
    mine = slot_ref[...] == slot
    pick_id = jnp.sum(jnp.where(mine, tok_ref[...].astype(jnp.float32), 0.0), axis=1, keepdims=True)
    fork = jnp.sum(jnp.where(mine, fork_ref[...].astype(jnp.float32), 0.0), axis=1, keepdims=True)
    fork_out[...] = jnp.broadcast_to(fork.astype(jnp.int32), fork_out.shape)
    cands = cq_ref.shape[0]
    pick = (
        lax.broadcasted_iota(jnp.int32, (padded, cands), 1).astype(jnp.float32) == pick_id
    ).astype(jnp.bfloat16)

    ones = jnp.ones((length, HEAD), jnp.bfloat16)
    for head in range(heads):
        lanes = slice(head * HEAD, (head + 1) * HEAD)
        picked = dot(pick, cq_ref[:, head * GROUP * HEAD : (head + 1) * GROUP * HEAD], (1, 0))
        branch_q = jnp.zeros((padded, HEAD), jnp.float32)
        for member in range(GROUP):
            chosen = (line >= member * owned) & (line < (member + 1) * owned)
            branch_q = jnp.where(chosen, picked[:, member * HEAD : (member + 1) * HEAD], branch_q)
        for member in range(GROUP):
            column = (head * GROUP + member) * HEAD
            qa_ref[head, member * rows : (member + 1) * rows, :] = q_ref[:, column : column + HEAD]
        qa_ref[head, GROUP * rows :, :] = branch_q.astype(jnp.bfloat16)

        reach = jnp.where(causal, row_sum[:, head : head + 1] - upto[head : head + 1, :], MASKED)
        decay = jnp.exp(reach) * SCALE
        branch_decay = jnp.exp(after[head : head + 1, :]) * SCALE
        raw = dot(qa_ref[head], k_ref[:, lanes], (1, 1))
        square = raw * raw
        weights = [
            (square[m * rows : (m + 1) * rows] * decay).astype(jnp.bfloat16) for m in range(GROUP)
        ]
        weights.append((square[GROUP * rows :] * branch_decay).astype(jnp.bfloat16))
        value = jnp.concatenate([v_ref[:, lanes], ones], axis=1)
        acc_ref[head] = dot(jnp.concatenate(weights, axis=0), value, (1, 0))

        new_k = dot(pick, ckv_ref[:, 0, lanes], (1, 0))
        new_v = dot(pick, ckv_ref[:, 1, lanes], (1, 0))
        inner = jnp.sum(branch_q * new_k, axis=1, keepdims=True)
        weight = inner * inner * SCALE
        own_ref[head, :, :HEAD] = weight * new_v
        own_ref[head, :, HEAD:] = jnp.broadcast_to(weight, (padded, HEAD))


def early_kernel(partners, late_partner, *refs):
    count = len(partners)
    qa_ref, acc_ref, own_ref, row_ref, fork_ref, gate_ref = refs[:6]
    near, far = refs[6 : 6 + count], refs[6 + count : 6 + 2 * count]
    (plain_ref, scaled_ref, late_row_ref, late_branch_ref, wp_ref, ws_ref, value_ref, key_ref) = refs[
        6 + 2 * count :
    ]
    ctx = lax.axis_index("ctx")
    first_core = lax.axis_index("feat") == 0
    rows = row_ref.shape[0]
    heads, total_rows, _ = qa_ref.shape
    padded = total_rows - GROUP * rows
    length = gate_ref.shape[1]
    half = length // 2
    blocks = [partner(ctx) for partner in partners]
    late = late_partner(ctx)
    fork = fork_ref[...]
    value_ref[:, HEAD:] = jnp.ones((value_ref.shape[0], HEAD), jnp.bfloat16)
    gates = [received_gates(ref, heads, first_core) for ref in near]
    zero = jnp.zeros((padded, length), jnp.float32)
    for head in range(heads):
        at = slice(head, head + 1)
        row_h = row_ref[:, at]
        own_total = gate_ref[at, :]
        for i in range(count):
            for j, ref in enumerate((near[i], far[i])):
                here = slice(i * length + j * half, i * length + (j + 1) * half)
                key_ref[here, :] = ref[head * half : (head + 1) * half, :]
                value_ref[here, :HEAD] = ref[(heads + head) * half : (heads + head + 1) * half, :]
        raw = dot(qa_ref[head], key_ref[...], (1, 1))
        square = raw * raw
        kept = zero
        late_row = jnp.zeros((1, length), jnp.float32)
        late_branch = jnp.where((ctx > late) & (ctx < fork), own_total, zero)
        for b, block in enumerate(blocks):
            after, total = gates[b][0][at, :], gates[b][1][at, :]
            kept = kept + jnp.where((block > ctx) & (block < fork), total, 0.0)
            late_row = late_row + jnp.where((block > late) & (block < ctx), total, 0.0)
            late_branch = late_branch + jnp.where((block > late) & (block < fork), total, 0.0)
            between = after
            past = after + jnp.where((ctx > block) & (ctx < fork), own_total, zero)
            for o, other in enumerate(blocks):
                if o != b:
                    step = gates[o][1][at, :]
                    between = between + jnp.where((other > block) & (other < ctx), step, 0.0)
                    past = past + jnp.where((other > block) & (other < fork), step, 0.0)
            decay = jnp.exp(jnp.where(block < ctx, row_h + between, MASKED)) * SCALE
            branch_decay = jnp.exp(jnp.where(block < fork, past, MASKED)) * SCALE
            crossed = (late > block) & (late < ctx)
            branch_crossed = (late > block) & (late < fork)
            cols = slice(b * length, (b + 1) * length)
            for ref, row_part, branch_part in (
                (wp_ref, jnp.where(crossed, 0.0, decay), jnp.where(branch_crossed, 0.0, branch_decay)),
                (ws_ref, jnp.where(crossed, decay, 0.0), jnp.where(branch_crossed, branch_decay, 0.0)),
            ):
                for member in range(GROUP):
                    span = slice(member * rows, (member + 1) * rows)
                    ref[span, cols] = (square[span, cols] * row_part).astype(jnp.bfloat16)
                ref[GROUP * rows :, cols] = (square[GROUP * rows :, cols] * branch_part).astype(
                    jnp.bfloat16
                )
        plain = dot(wp_ref[...], value_ref[...], (1, 0))
        scaled = dot(ws_ref[...], value_ref[...], (1, 0))
        split = GROUP * rows
        plain_ref[head, :split] = plain[:split] + acc_ref[head, :split, :]
        scaled_ref[head, :split] = scaled[:split]
        keep = jnp.exp(jnp.where(ctx < fork, kept, MASKED))
        crossed = (late > ctx) & (late < fork)
        before = acc_ref[head, split:, :]
        for side in range(2):
            part = slice(side * HEAD, (side + 1) * HEAD)
            moved = keep * before[:, part]
            plain_ref[head, split:, part] = (
                plain[split:, part] + own_ref[head, :, part] + jnp.where(crossed, 0.0, moved)
            )
            scaled_ref[head, split:, part] = scaled[split:, part] + jnp.where(crossed, moved, 0.0)
        late_row_ref[at, :] = jnp.where(late < ctx, late_row, MASKED)
        late_branch_ref[head] = jnp.where(late < fork, late_branch, MASKED)


def half_product(qa, ref, head, heads, rows, row_part, branch_part):
    half = row_part.shape[1]
    raw = dot(qa, ref[head * half : (head + 1) * half, :], (1, 1))
    square = raw * raw
    weights = [
        (square[m * rows : (m + 1) * rows] * row_part).astype(jnp.bfloat16) for m in range(GROUP)
    ]
    weights.append((square[GROUP * rows :] * branch_part).astype(jnp.bfloat16))
    value = ref[(heads + head) * half : (heads + head + 1) * half, :]
    value = jnp.concatenate([value, jnp.ones((half, HEAD), jnp.bfloat16)], axis=1)
    return dot(jnp.concatenate(weights, axis=0), value, (1, 0))


def near_kernel(
    qa_ref, row_ref, plain_ref, scaled_ref, late_row_ref, late_branch_ref, near_ref,
    sum_ref, decay_ref, branch_decay_ref,
):
    heads = qa_ref.shape[0]
    rows = row_ref.shape[0]
    half = decay_ref.shape[2]
    first_core = lax.axis_index("feat") == 0
    after, total = received_gates(near_ref, heads, first_core)
    factor = jnp.exp(total)
    for head in range(heads):
        at = slice(head, head + 1)
        decay = jnp.exp(row_ref[:, at] + (late_row_ref[at, :] + after[at, :])) * SCALE
        branch_decay = jnp.exp(late_branch_ref[head] + after[at, :]) * SCALE
        decay_ref[head] = decay[:, half:]
        branch_decay_ref[head] = branch_decay[:, half:]
        part = half_product(
            qa_ref[head], near_ref, head, heads, rows, decay[:, :half], branch_decay[:, :half]
        )
        for side in range(2):
            cols = slice(side * HEAD, (side + 1) * HEAD)
            sum_ref[head, :, cols] = part[:, cols] + (
                plain_ref[head, :, cols] + factor[at, :] * scaled_ref[head, :, cols]
            )


def final_kernel(
    qa_ref, sum_ref, decay_ref, branch_decay_ref, far_ref, out_ref, branch_ref,
    stage_ref, branch_stage_ref, line_ref, sem,
):
    heads = qa_ref.shape[0]
    rows = out_ref.shape[0]
    owned = branch_ref.shape[0]
    split = GROUP * rows
    copies = []
    for head in range(heads):
        total = sum_ref[head] + half_product(
            qa_ref[head], far_ref, head, heads, rows, decay_ref[head], branch_decay_ref[head]
        )
        ratio = total[:, :HEAD] / jnp.maximum(total[:, HEAD:], 1.0)
        line_ref[...] = ratio[split:]
        for member in range(GROUP):
            column = (head * GROUP + member) * HEAD
            lanes = slice(column, column + HEAD)
            stage_ref[:, lanes] = ratio[member * rows : (member + 1) * rows].astype(out_ref.dtype)
            branch_stage_ref[:, lanes] = line_ref[
                member * owned : (member + 1) * owned, :
            ].astype(branch_ref.dtype)
        wide = pl.ds(head * GROUP * HEAD, GROUP * HEAD)
        copies.append(
            pltpu.make_async_copy(stage_ref.at[:, wide], out_ref.at[:, wide], sem.at[head])
        )
        copies[-1].start()
    copies.append(pltpu.make_async_copy(branch_stage_ref, branch_ref, sem.at[heads]))
    copies[-1].start()
    for copy in copies:
        copy.wait()


def swaps(count):
    if count & (count - 1) == 0:
        return [
            ([(i, i ^ step) for i in range(count)], functools.partial(lambda s, i: i ^ s, step))
            for step in range(1, count)
        ]
    return [
        (
            [(i, (i + step) % count) for i in range(count)],
            functools.partial(lambda s, i: lax.rem(i + count - s, count), step),
        )
        for step in range(1, count)
    ]


ORDER = (2, 1, 3)


def call(kernel, operands, outs, scratch=(), vmem=16 << 20, results=None, inputs=None):
    spec = pl.BlockSpec(memory_space=pltpu.VMEM)
    return pl.pallas_call(
        kernel,
        out_shape=outs,
        in_specs=inputs or [spec] * len(operands),
        out_specs=results or (spec,) * len(outs),
        scratch_shapes=list(scratch),
        compiler_params=pltpu.CompilerParams(vmem_limit_bytes=vmem),
        cost_estimate=pl.CostEstimate(flops=1 << 29, bytes_accessed=4 << 20, transcendentals=0),
    )(*operands)


def per_device(queries, keys, values, log_gate, cand_q, cand_kv, token_ids, fork_pos, slot_map):
    n_ctx = lax.axis_size("ctx")
    n_feat = lax.axis_size("feat")
    length, width = keys.shape
    heads = width // HEAD
    rows = length // n_feat
    half = length // 2
    branches = token_ids.shape[0]
    owned = branches // (n_ctx * n_feat)
    padded = -(-GROUP * owned // 16) * 16
    total_rows = GROUP * rows + padded
    assert n_feat == 2 and length == HEAD
    f32, bf16 = jnp.float32, jnp.bfloat16
    shape = jax.ShapeDtypeStruct

    hbm = pl.BlockSpec(memory_space=pltpu.HBM)
    in_hbm = lambda x: pltpu.with_memory_space_constraint(x, pltpu.HBM)
    gates = in_hbm(log_gate.T)
    (payload,) = call(
        pack_kernel, [in_hbm(keys), in_hbm(values), gates],
        (shape((2 * heads * half + gate_rows(heads), HEAD), bf16),),
        [pltpu.VMEM(gates.shape, f32), pltpu.SemaphoreType.DMA((1 + 2 * heads,))],
        vmem=4 << 20, inputs=[hbm] * 3,
    )
    pairings = swaps(n_ctx)
    count = len(pairings)
    steps = [s - 1 for s in ORDER] if count == 3 else list(range(count))
    near, far = [], []
    for s in steps:
        near.append(lax.ppermute(payload, "ctx", pairings[s][0]))
    for part in near:
        far.append(lax.ppermute(part, "feat", [(0, 1), (1, 0)]))
    partners = [pairings[s][1] for s in steps]

    sources = [
        queries, keys, values, gates, cand_q, cand_kv,
        token_ids[None], fork_pos[None], slot_map[None],
    ]
    wide = shape((heads, total_rows, 2 * HEAD), f32)
    queries_all, acc, token, row_sum, fork, total = call(
        functools.partial(own_kernel, n_feat), [in_hbm(s) for s in sources],
        (
            shape((heads, total_rows, HEAD), bf16),
            wide,
            shape((heads, padded, 2 * HEAD), f32),
            shape((rows, heads), f32),
            shape((padded, length), jnp.int32),
            shape((heads, length), f32),
        ),
        [pltpu.VMEM((rows, queries.shape[1]), queries.dtype)]
        + [pltpu.VMEM(s.shape, s.dtype) for s in sources[1:]]
        + [pltpu.SemaphoreType.DMA((len(sources),))],
        inputs=[hbm] * len(sources),
    )
    early = (count - 1) * length
    plain, scaled, late_row, late_branch = call(
        functools.partial(early_kernel, partners[:-1], partners[-1]),
        [queries_all, acc, token, row_sum, fork, total, *near[:-1], *far[:-1]],
        (wide, wide, shape((heads, length), f32), shape((heads, padded, length), f32)),
        [
            pltpu.VMEM((total_rows, early), bf16),
            pltpu.VMEM((total_rows, early), bf16),
            pltpu.VMEM((early, 2 * HEAD), bf16),
            pltpu.VMEM((early, HEAD), bf16),
        ],
    )
    sums, decay, branch_decay = call(
        near_kernel,
        [queries_all, row_sum, plain, scaled, late_row, late_branch, near[-1]],
        (wide, shape((heads, rows, half), f32), shape((heads, padded, half), f32)),
    )
    return call(
        final_kernel, [queries_all, sums, decay, branch_decay, far[-1]],
        (shape((rows, queries.shape[1]), bf16), shape((owned, queries.shape[1]), bf16)),
        [
            pltpu.VMEM((rows, queries.shape[1]), bf16),
            pltpu.VMEM((owned, queries.shape[1]), bf16),
            pltpu.VMEM((padded, HEAD), f32),
            pltpu.SemaphoreType.DMA((heads + 1,)),
        ],
        results=(hbm, hbm),
    )


def solution(mesh):
    return sharded(mesh)


def sharded(mesh):
    return jax.shard_map(
        per_device,
        mesh=mesh,
        in_specs=(
            P(("groups", "ctx"), "head"),
            P(("groups", "ctx"), "head"),
            P(("groups", "ctx"), "head"),
            P(("groups", "ctx"), "head"),
            P("groups", "head"),
            P("groups", None, "head"),
            P("groups"),
            P("groups"),
            P("groups"),
        ),
        out_specs=(P(("groups", "ctx", "feat"), "head"), P(("groups", "ctx", "feat"), "head")),
        check_vma=False,
    )
```

time: 23.6 us -> 23.5 us (level)
  the two profiles are of different devices: /device:TPU:0 before, /device:TPU:17 now
where the time goes in v3:
time: 23.5 us; the launch traced here: 23.3 us
  waiting for transfers between devices  7.79 us (33%)
  starting transfers between devices  7.69 us (33%)
  Pallas kernels  7.12 us (30%)
  between operations  0.69 us (3%)
    ppermute x3, waiting for transfers between devices, per_device(): near.append(lax.ppermute(payload, 'ctx', pairings[s][0]))  7.78 us
    pallas_call x5, Pallas kernels, call(): pl.pallas_call(kernel, out_shape=outs, in_specs=inputs or [spec] * len(op...  7.12 us
    ppermute x3, starting transfers between devices, per_device(): far.append(lax.ppermute(part, 'feat', [(0, 1), (1, 0)]))  4.98 us
    ppermute x3, starting transfers between devices, per_device(): near.append(lax.ppermute(payload, 'ctx', pairings[s][0]))  2.71 us
  transfers between devices with their start and end apart: 6, of which 2 were waited for; matrix products, arithmetic and copies ran while one was open for 0% of the time, Pallas kernels for 20%

profile of v3, /device:TPU:17, one launch (start us, length us, event | category | flops | bytes accessed | tf_op | source)
XLA Modules:
  0.0 23.3 jit_solution(16150096589030062353)
XLA Ops:
  0.6 0.9 %shard_map.105 = bf16[520,128]{1,0:T(8,128)(2,1)S(1)} custom-call(bf16[128,512]{1,0:T(8,128)(2,1)} %k_ref.1, bf16[128,512]{1,0:T(8,128)(2,1)} %v_ref.1, f32[4,128]{1,0:T(4,128)} %bitcast.4), custom_call_target="tpu_custom_call" | custom-call | flops 536870912 | bytes 4194304 | tf_op jit(solution)/shard_map/pallas_call | solution.py:333
  1.6 0.1 collective-permute-start
  1.7 1.4 %collective-permute-start.1 = (bf16[520,128]{1,0:T(8,128)(2,1)S(1)}, bf16[520,128]{1,0:T(8,128)(2,1)S(1)}, u32[]{:S(2)}, u32[]{:S(2)}) collective-permute-start(bf16[520,128]{1,0:T(8,128)(2,1)S(1)} %shard_map.105), channel_id=1, source_target_pairs={{0,4},{4,0},{8,12},{12,8},{1,5},{5,1},{9,13},{13,9},{2,6},{6,2},{1... | collective-permute-start | bytes 399368 | tf_op jit(solution)/shard_map/ppermute | solution.py:373
  3.0 1.3 %collective-permute-start.4 = (bf16[520,128]{1,0:T(8,128)(2,1)S(1)}, bf16[520,128]{1,0:T(8,128)(2,1)S(1)}, u32[]{:S(2)}, u32[]{:S(2)}) collective-permute-start(bf16[520,128]{1,0:T(8,128)(2,1)S(1)} %shard_map.105), channel_id=1, source_target_pairs={{0,12},{4,8},{8,4},{12,0},{1,13},{5,9},{9,5},{13,1},{2,14},{6,10},... | collective-permute-start | bytes 399368 | tf_op jit(solution)/shard_map/ppermute | solution.py:373
  4.3 2.7 %collective-permute-done.refs_6_ = bf16[520,128]{1,0:T(8,128)(2,1)S(1)} collective-permute-done((bf16[520,128]{1,0:T(8,128)(2,1)S(1)}, bf16[520,128]{1,0:T(8,128)(2,1)S(1)}, u32[]{:S(2)}, u32[]{:S(2)}) %collective-permute-start) | collective-permute-done | bytes 133152 | tf_op jit(solution)/shard_map/ppermute | solution.py:373
  7.0 2.7 %collective-permute-start.2 = (bf16[520,128]{1,0:T(8,128)(2,1)S(1)}, bf16[520,128]{1,0:T(8,128)(2,1)S(1)}, u32[]{:S(2)}, u32[]{:S(2)}) collective-permute-start(bf16[520,128]{1,0:T(8,128)(2,1)S(1)} %collective-permute-done.refs_6_), channel_id=1, source_target_pairs={{0,1},{1,0},{2,3},{3,2},{4,5},{5,4},{6,7},{7,6},{8,9},{9,8},{10,11... | collective-permute-start | bytes 399368 | tf_op jit(solution)/shard_map/ppermute | solution.py:375
  9.7 0.0 collective-permute-done.1.refs_7_
  9.7 1.8 %collective-permute-start.3 = (bf16[520,128]{1,0:T(8,128)(2,1)S(1)}, bf16[520,128]{1,0:T(8,128)(2,1)S(1)}, u32[]{:S(2)}, u32[]{:S(2)}) collective-permute-start(bf16[520,128]{1,0:T(8,128)(2,1)S(1)} %collective-permute-done.1.refs_7_), channel_id=1, source_target_pairs={{0,1},{1,0},{2,3},{3,2},{4,5},{5,4},{6,7},{7,6},{8,9},{9,8},{10,11... | collective-permute-start | bytes 399368 | tf_op jit(solution)/shard_map/ppermute | solution.py:375
  11.5 5.1 %collective-permute-done.4.near_ref = bf16[520,128]{1,0:T(8,128)(2,1)S(1)} collective-permute-done((bf16[520,128]{1,0:T(8,128)(2,1)S(1)}, bf16[520,128]{1,0:T(8,128)(2,1)S(1)}, u32[]{:S(2)}, u32[]{:S(2)}) %collective-permute-start.4) | collective-permute-done | bytes 133152 | tf_op jit(solution)/shard_map/ppermute | solution.py:373
  16.6 0.5 %collective-permute-start.5 = (bf16[520,128]{1,0:T(8,128)(2,1)S(1)}, bf16[520,128]{1,0:T(8,128)(2,1)S(1)}, u32[]{:S(2)}, u32[]{:S(2)}) collective-permute-start(bf16[520,128]{1,0:T(8,128)(2,1)S(1)} %collective-permute-done.4.near_ref), channel_id=1, source_target_pairs={{0,1},{1,0},{2,3},{3,2},{4,5},{5,4},{6,7},{7,6},{8,9},{9,8},{10,11... | collective-permute-start | bytes 399368 | tf_op jit(solution)/shard_map/ppermute | solution.py:375
  17.1 2.8 %shard_map.104 = (bf16[4,336,128]{2,1,0:T(8,128)(2,1)S(1)}, f32[4,336,256]{2,1,0:T(8,128)S(1)}, f32[4,16,256]{2,1,0:T(8,128)S(1)}, f32[64,4]{1,0:T(8,128)S(1)}, ...) custom-call(bf16[128,2560]{1,0:T(8,128)(2,1)} %refs_0_.1, bf16[128,512]{1,0:T(8,128)(2,1)} %k_ref.1, bf16[128,512]{1,0:T(8,128)(2,1)} %v_ref.1, ...), custom_call_target="tpu_custom_call" | custom-call | flops 536870912 | bytes 4194304 | tf_op jit(solution)/shard_map/pallas_call | solution.py:333
  19.8 0.0 collective-permute-done.2.refs_8_
  19.9 0.0 collective-permute-done.3.refs_9_
  19.9 1.2 %shard_map.106 = (f32[4,336,256]{2,1,0:T(8,128)S(1)}, f32[4,336,256]{2,1,0:T(8,128)S(1)}, f32[4,128]{1,0:T(4,128)S(1)}, f32[4,16,128]{2,1,0:T(8,128)S(1)}) custom-call(bf16[4,336,128]{2,1,0:T(8,128)(2,1)S(1)} %get-tuple-element.15.refs_0_.qa_ref, f32[4,336,256]{2,1,0:T(8,128)S(1)} %get-tuple-element.17.refs_1_, f32[4,16,256]{2,1,0:T(8,128)S(1)} %get-tuple-element.18.refs_2_, ...), custom_call_target="tpu_custom_call" | custom-call | flops 536870912 | bytes 4194304 | tf_op jit(solution)/shard_map/pallas_call | solution.py:333
  21.1 0.8 %shard_map.107 = (f32[4,336,256]{2,1,0:T(8,128)S(1)}, f32[4,64,64]{2,1,0:T(8,128)S(1)}, f32[4,16,64]{2,1,0:T(8,128)S(1)}) custom-call(bf16[4,336,128]{2,1,0:T(8,128)(2,1)S(1)} %get-tuple-element.15.refs_0_.qa_ref, f32[64,4]{1,0:T(8,128)S(1)} %get-tuple-element.16.refs_3_.row_ref, f32[4,336,256]{2,1,0:T(8,128)S(1)} %get-tuple-element.21.plain_ref, ...), custom_call_target="tpu_custom_call" | custom-call | flops 536870912 | bytes 4194304 | tf_op jit(solution)/shard_map/pallas_call | solution.py:333
  21.9 0.0 collective-permute-done.5.far_ref
  21.9 1.4 %shard_map.108 = (bf16[64,2560]{1,0:T(8,128)(2,1)}, bf16[2,2560]{1,0:T(2,128)(2,1)}) custom-call(bf16[4,336,128]{2,1,0:T(8,128)(2,1)S(1)} %get-tuple-element.15.refs_0_.qa_ref, f32[4,336,256]{2,1,0:T(8,128)S(1)} %get-tuple-element.25.sum_ref, f32[4,64,64]{2,1,0:T(8,128)S(1)} %get-tuple-element.26.decay_ref, ...), custom_call_target="tpu_custom_call" | custom-call | flops 536870912 | bytes 4194304 | tf_op jit(solution)/shard_map/pallas_call | solution.py:333
Async XLA Ops:
  1.6 5.4 %collective-permute-start = (bf16[520,128]{1,0:T(8,128)(2,1)S(1)}, bf16[520,128]{1,0:T(8,128)(2,1)S(1)}, u32[]{:S(2)}, u32[]{:S(2)}) collective-permute-start(bf16[520,128]{1,0:T(8,128)(2,1)S(1)} %shard_map.105), channel_id=1, source_target_pairs={{0,8},{4,12},{8,0},{12,4},{1,9},{5,13},{9,1},{13,5},{2,10},{6,14},... | collective-permute-start | bytes 399368 | tf_op jit(solution)/shard_map/ppermute | solution.py:373
  1.7 8.0 %collective-permute-start.1 = (bf16[520,128]{1,0:T(8,128)(2,1)S(1)}, bf16[520,128]{1,0:T(8,128)(2,1)S(1)}, u32[]{:S(2)}, u32[]{:S(2)}) collective-permute-start(bf16[520,128]{1,0:T(8,128)(2,1)S(1)} %shard_map.105), channel_id=1, source_target_pairs={{0,4},{4,0},{8,12},{12,8},{1,5},{5,1},{9,13},{13,9},{2,6},{6,2},{1... | collective-permute-start | bytes 399368 | tf_op jit(solution)/shard_map/ppermute | solution.py:373
  3.0 13.5 %collective-permute-start.4 = (bf16[520,128]{1,0:T(8,128)(2,1)S(1)}, bf16[520,128]{1,0:T(8,128)(2,1)S(1)}, u32[]{:S(2)}, u32[]{:S(2)}) collective-permute-start(bf16[520,128]{1,0:T(8,128)(2,1)S(1)} %shard_map.105), channel_id=1, source_target_pairs={{0,12},{4,8},{8,4},{12,0},{1,13},{5,9},{9,5},{13,1},{2,14},{6,10},... | collective-permute-start | bytes 399368 | tf_op jit(solution)/shard_map/ppermute | solution.py:373
  7.0 12.9 %collective-permute-start.2 = (bf16[520,128]{1,0:T(8,128)(2,1)S(1)}, bf16[520,128]{1,0:T(8,128)(2,1)S(1)}, u32[]{:S(2)}, u32[]{:S(2)}) collective-permute-start(bf16[520,128]{1,0:T(8,128)(2,1)S(1)} %collective-permute-done.refs_6_), channel_id=1, source_target_pairs={{0,1},{1,0},{2,3},{3,2},{4,5},{5,4},{6,7},{7,6},{8,9},{9,8},{10,11... | collective-permute-start | bytes 399368 | tf_op jit(solution)/shard_map/ppermute | solution.py:375
  9.7 10.2 %collective-permute-start.3 = (bf16[520,128]{1,0:T(8,128)(2,1)S(1)}, bf16[520,128]{1,0:T(8,128)(2,1)S(1)}, u32[]{:S(2)}, u32[]{:S(2)}) collective-permute-start(bf16[520,128]{1,0:T(8,128)(2,1)S(1)} %collective-permute-done.1.refs_7_), channel_id=1, source_target_pairs={{0,1},{1,0},{2,3},{3,2},{4,5},{5,4},{6,7},{7,6},{8,9},{9,8},{10,11... | collective-permute-start | bytes 399368 | tf_op jit(solution)/shard_map/ppermute | solution.py:375
  16.6 5.3 %collective-permute-start.5 = (bf16[520,128]{1,0:T(8,128)(2,1)S(1)}, bf16[520,128]{1,0:T(8,128)(2,1)S(1)}, u32[]{:S(2)}, u32[]{:S(2)}) collective-permute-start(bf16[520,128]{1,0:T(8,128)(2,1)S(1)} %collective-permute-done.4.near_ref), channel_id=1, source_target_pairs={{0,1},{1,0},{2,3},{3,2},{4,5},{5,4},{6,7},{7,6},{8,9},{9,8},{10,11... | collective-permute-start | bytes 399368 | tf_op jit(solution)/shard_map/ppermute | solution.py:375

commit v4 on v3

--- a/solution.py
+++ b/solution.py
@@ -31,19 +31,13 @@
     return keep(row, col).astype(jnp.float32)
 
 
-def from_inclusive(inclusive):
-    lane = lax.broadcasted_iota(jnp.int32, inclusive.shape, 1)
-    last = inclusive.shape[1] - 1
-    after = jnp.where(lane == last, 0.0, pltpu.roll(inclusive, last, 1))
-    total = jnp.broadcast_to(inclusive[:, :1], inclusive.shape)
-    return after, total
-
-
 def received_gates(ref, heads, first_core):
     tile = ref[ref.shape[0] - gate_rows(heads) :, :].astype(jnp.float32)
-    mixed = tile + pltpu.roll(tile, tile.shape[0] - heads, 0)
-    after, total = from_inclusive(mixed)
-    after = jnp.where(first_core, after, pltpu.roll(after, after.shape[1] // 2, 1))
+    gate = tile + pltpu.roll(tile, tile.shape[0] - heads, 0)
+    length = gate.shape[1]
+    after = exact_dot(gate, triangle(length, lambda r, c: r > c), (1, 0))
+    total = exact_dot(gate, triangle(length, lambda r, c: r >= 0), (1, 0))
+    after = jnp.where(first_core, after, pltpu.roll(after, length // 2, 1))
     return after, total
 
 
@@ -71,9 +65,9 @@
     for copy in copies:
         copy.start()
     gates.wait()
-    inclusive = exact_dot(gate_ref[...], triangle(length, lambda r, c: r >= c), (1, 0))
-    high = inclusive.astype(jnp.bfloat16).astype(jnp.float32)
-    parts = [high, inclusive - high]
+    gate = gate_ref[...]
+    high = gate.astype(jnp.bfloat16).astype(jnp.float32)
+    parts = [high, gate - high]
     spare = gate_rows(heads) - 2 * heads
     if spare:
         parts.append(jnp.zeros((spare, length), jnp.float32))
@@ -158,156 +152,250 @@
         own_ref[head, :, HEAD:] = jnp.broadcast_to(weight, (padded, HEAD))
 
 
+def weigh(square, row_part, branch_part, rows):
+    members = (square.shape[0] - branch_part.shape[0]) // rows
+    parts = [square[m * rows : (m + 1) * rows] * row_part for m in range(members)]
+    parts.append(square[members * rows :] * branch_part)
+    return jnp.concatenate(parts, axis=0).astype(jnp.bfloat16)
+
+
 def early_kernel(partners, late_partner, *refs):
     count = len(partners)
     qa_ref, acc_ref, own_ref, row_ref, fork_ref, gate_ref = refs[:6]
     near, far = refs[6 : 6 + count], refs[6 + count : 6 + 2 * count]
-    (plain_ref, scaled_ref, late_row_ref, late_branch_ref, wp_ref, ws_ref, value_ref, key_ref) = refs[
-        6 + 2 * count :
-    ]
+    (
+        plain_ref, scaled_ref, late_row_ref, late_branch_ref, out_ref, value_ref, key_ref, stage_ref,
+        sem,
+    ) = refs[6 + 2 * count :]
     ctx = lax.axis_index("ctx")
     first_core = lax.axis_index("feat") == 0
     rows = row_ref.shape[0]
     heads, total_rows, _ = qa_ref.shape
-    padded = total_rows - GROUP * rows
+    split = GROUP * rows
+    padded = total_rows - split
     length = gate_ref.shape[1]
     half = length // 2
     blocks = [partner(ctx) for partner in partners]
     late = late_partner(ctx)
     fork = fork_ref[...]
-    value_ref[:, HEAD:] = jnp.ones((value_ref.shape[0], HEAD), jnp.bfloat16)
+    value_ref[:, :, HEAD:] = jnp.ones((heads, count * length, HEAD), jnp.bfloat16)
     gates = [received_gates(ref, heads, first_core) for ref in near]
     zero = jnp.zeros((padded, length), jnp.float32)
     for head in range(heads):
-        at = slice(head, head + 1)
-        row_h = row_ref[:, at]
-        own_total = gate_ref[at, :]
         for i in range(count):
             for j, ref in enumerate((near[i], far[i])):
                 here = slice(i * length + j * half, i * length + (j + 1) * half)
-                key_ref[here, :] = ref[head * half : (head + 1) * half, :]
-                value_ref[here, :HEAD] = ref[(heads + head) * half : (heads + head + 1) * half, :]
-        raw = dot(qa_ref[head], key_ref[...], (1, 1))
-        square = raw * raw
-        kept = zero
-        late_row = jnp.zeros((1, length), jnp.float32)
-        late_branch = jnp.where((ctx > late) & (ctx < fork), own_total, zero)
-        for b, block in enumerate(blocks):
-            after, total = gates[b][0][at, :], gates[b][1][at, :]
-            kept = kept + jnp.where((block > ctx) & (block < fork), total, 0.0)
-            late_row = late_row + jnp.where((block > late) & (block < ctx), total, 0.0)
-            late_branch = late_branch + jnp.where((block > late) & (block < fork), total, 0.0)
-            between = after
-            past = after + jnp.where((ctx > block) & (ctx < fork), own_total, zero)
-            for o, other in enumerate(blocks):
-                if o != b:
-                    step = gates[o][1][at, :]
-                    between = between + jnp.where((other > block) & (other < ctx), step, 0.0)
-                    past = past + jnp.where((other > block) & (other < fork), step, 0.0)
-            decay = jnp.exp(jnp.where(block < ctx, row_h + between, MASKED)) * SCALE
-            branch_decay = jnp.exp(jnp.where(block < fork, past, MASKED)) * SCALE
-            crossed = (late > block) & (late < ctx)
-            branch_crossed = (late > block) & (late < fork)
-            cols = slice(b * length, (b + 1) * length)
-            for ref, row_part, branch_part in (
-                (wp_ref, jnp.where(crossed, 0.0, decay), jnp.where(branch_crossed, 0.0, branch_decay)),
-                (ws_ref, jnp.where(crossed, decay, 0.0), jnp.where(branch_crossed, branch_decay, 0.0)),
-            ):
-                for member in range(GROUP):
-                    span = slice(member * rows, (member + 1) * rows)
-                    ref[span, cols] = (square[span, cols] * row_part).astype(jnp.bfloat16)
-                ref[GROUP * rows :, cols] = (square[GROUP * rows :, cols] * branch_part).astype(
-                    jnp.bfloat16
+                key_ref[head, here, :] = ref[head * half : (head + 1) * half, :]
+                value_ref[head, here, :HEAD] = ref[
+                    (heads + head) * half : (heads + head + 1) * half, :
+                ]
+
+    def body(first):
+        raws = [dot(qa_ref[head, first:], key_ref[head], (1, 1)) for head in range(heads)]
+        weights = []
+        keeps = []
+        for head in range(heads):
+            at = slice(head, head + 1)
+            row_h = row_ref[:, at]
+            own_total = gate_ref[at, :]
+            square = raws[head] * raws[head]
+            kept = zero
+            late_row = jnp.zeros((1, length), jnp.float32)
+            late_branch = jnp.where((ctx > late) & (ctx < fork), own_total, zero)
+            plains, scaleds = [], []
+            for b, block in enumerate(blocks):
+                after, total = gates[b][0][at, :], gates[b][1][at, :]
+                kept = kept + jnp.where((block > ctx) & (block < fork), total, 0.0)
+                late_row = late_row + jnp.where((block > late) & (block < ctx), total, 0.0)
+                late_branch = late_branch + jnp.where((block > late) & (block < fork), total, 0.0)
+                between = after
+                past = after + jnp.where((ctx > block) & (ctx < fork), own_total, zero)
+                for o, other in enumerate(blocks):
+                    if o != b:
+                        step = gates[o][1][at, :]
+                        between = between + jnp.where((other > block) & (other < ctx), step, 0.0)
+                        past = past + jnp.where((other > block) & (other < fork), step, 0.0)
+                branch_decay = jnp.exp(jnp.where(block < fork, past, MASKED)) * SCALE
+                crossed = (late > block) & (late < ctx)
+                branch_crossed = (late > block) & (late < fork)
+                decay = None
+                if first == 0:
+                    decay = jnp.exp(jnp.where(block < ctx, row_h + between, MASKED)) * SCALE
+                part = square[:, b * length : (b + 1) * length]
+                plains.append(
+                    weigh(
+                        part,
+                        None if decay is None else jnp.where(crossed, 0.0, decay),
+                        jnp.where(branch_crossed, 0.0, branch_decay),
+                        rows,
+                    )
                 )
-        plain = dot(wp_ref[...], value_ref[...], (1, 0))
-        scaled = dot(ws_ref[...], value_ref[...], (1, 0))
-        split = GROUP * rows
-        plain_ref[head, :split] = plain[:split] + acc_ref[head, :split, :]
-        scaled_ref[head, :split] = scaled[:split]
-        keep = jnp.exp(jnp.where(ctx < fork, kept, MASKED))
+                scaleds.append(
+                    weigh(
+                        part,
+                        None if decay is None else jnp.where(crossed, decay, 0.0),
+                        jnp.where(branch_crossed, branch_decay, 0.0),
+                        rows,
+                    )
+                )
+            weights.append((jnp.concatenate(plains, axis=1), jnp.concatenate(scaleds, axis=1)))
+            keeps.append(jnp.exp(jnp.where(ctx < fork, kept, MASKED)))
+            late_row_ref[at, :] = jnp.where(late < ctx, late_row, MASKED)
+            late_branch_ref[head] = jnp.where(late < fork, late_branch, MASKED)
         crossed = (late > ctx) & (late < fork)
-        before = acc_ref[head, split:, :]
-        for side in range(2):
-            part = slice(side * HEAD, (side + 1) * HEAD)
-            moved = keep * before[:, part]
-            plain_ref[head, split:, part] = (
-                plain[split:, part] + own_ref[head, :, part] + jnp.where(crossed, 0.0, moved)
-            )
-            scaled_ref[head, split:, part] = scaled[split:, part] + jnp.where(crossed, moved, 0.0)
-        late_row_ref[at, :] = jnp.where(late < ctx, late_row, MASKED)
-        late_branch_ref[head] = jnp.where(late < fork, late_branch, MASKED)
-
-
-def half_product(qa, ref, head, heads, rows, row_part, branch_part):
-    half = row_part.shape[1]
-    raw = dot(qa, ref[head * half : (head + 1) * half, :], (1, 1))
-    square = raw * raw
+        for head in range(heads):
+            plain, scaled = [dot(w, value_ref[head], (1, 0)) for w in weights[head]]
+            if first == 0:
+                plain_ref[head, :split] = plain[:split] + acc_ref[head, :split, :]
+                scaled_ref[head, :split] = scaled[:split]
+            before = acc_ref[head, split:, :]
+            for side in range(2):
+                cols = slice(side * HEAD, (side + 1) * HEAD)
+                moved = keeps[head] * before[:, cols]
+                plain_ref[head, split:, cols] = (
+                    plain[split - first :, cols]
+                    + own_ref[head, :, cols]
+                    + jnp.where(crossed, 0.0, moved)
+                )
+                scaled_ref[head, split:, cols] = scaled[split - first :, cols] + jnp.where(
+                    crossed, moved, 0.0
+                )
+
+    needed = functools.reduce(jnp.logical_or, [block < ctx for block in blocks])
+    pl.when(needed)(functools.partial(body, 0))
+    pl.when(jnp.logical_not(needed))(functools.partial(body, split))
+
+    def finish(ref):
+        for head in range(heads):
+            put_rows(head, ref[head, :split], stage_ref, out_ref, sem).start()
+        for head in range(heads):
+            rows_copy(head, stage_ref, out_ref, sem).wait()
+
+    pl.when(needed & (late > ctx))(functools.partial(finish, plain_ref))
+    pl.when(jnp.logical_not(needed) & (late > ctx))(functools.partial(finish, acc_ref))
+
+
+def rows_copy(head, stage_ref, out_ref, sem):
+    wide = pl.ds(head * GROUP * HEAD, GROUP * HEAD)
+    return pltpu.make_async_copy(stage_ref.at[:, wide], out_ref.at[:, wide], sem.at[head])
+
+
+def put_rows(head, total, stage_ref, out_ref, sem):
+    rows = stage_ref.shape[0]
+    ratio = total[:, :HEAD] / jnp.maximum(total[:, HEAD:], 1.0)
+    for member in range(GROUP):
+        column = (head * GROUP + member) * HEAD
+        stage_ref[:, column : column + HEAD] = ratio[member * rows : (member + 1) * rows].astype(
+            stage_ref.dtype
+        )
+    return rows_copy(head, stage_ref, out_ref, sem)
+
+
+def half_products(qa_ref, ref, first, row_parts, branch_parts, rows):
+    heads = qa_ref.shape[0]
+    half = branch_parts[0].shape[1]
+    raws = [
+        dot(qa_ref[head, first:], ref[head * half : (head + 1) * half, :], (1, 1))
+        for head in range(heads)
+    ]
     weights = [
-        (square[m * rows : (m + 1) * rows] * row_part).astype(jnp.bfloat16) for m in range(GROUP)
+        weigh(raws[head] * raws[head], row_parts[head], branch_parts[head], rows)
+        for head in range(heads)
     ]
-    weights.append((square[GROUP * rows :] * branch_part).astype(jnp.bfloat16))
-    value = ref[(heads + head) * half : (heads + head + 1) * half, :]
-    value = jnp.concatenate([value, jnp.ones((half, HEAD), jnp.bfloat16)], axis=1)
-    return dot(jnp.concatenate(weights, axis=0), value, (1, 0))
+    ones = jnp.ones((half, HEAD), jnp.bfloat16)
+    sums = []
+    for head in range(heads):
+        value = ref[(heads + head) * half : (heads + head + 1) * half, :]
+        sums.append(dot(weights[head], jnp.concatenate([value, ones], axis=1), (1, 0)))
+    return sums
 
 
 def near_kernel(
+    late_partner,
     qa_ref, row_ref, plain_ref, scaled_ref, late_row_ref, late_branch_ref, near_ref,
     sum_ref, decay_ref, branch_decay_ref,
 ):
     heads = qa_ref.shape[0]
     rows = row_ref.shape[0]
     half = decay_ref.shape[2]
+    ctx = lax.axis_index("ctx")
     first_core = lax.axis_index("feat") == 0
     after, total = received_gates(near_ref, heads, first_core)
     factor = jnp.exp(total)
-    for head in range(heads):
-        at = slice(head, head + 1)
-        decay = jnp.exp(row_ref[:, at] + (late_row_ref[at, :] + after[at, :])) * SCALE
-        branch_decay = jnp.exp(late_branch_ref[head] + after[at, :]) * SCALE
-        decay_ref[head] = decay[:, half:]
-        branch_decay_ref[head] = branch_decay[:, half:]
-        part = half_product(
-            qa_ref[head], near_ref, head, heads, rows, decay[:, :half], branch_decay[:, :half]
-        )
-        for side in range(2):
-            cols = slice(side * HEAD, (side + 1) * HEAD)
-            sum_ref[head, :, cols] = part[:, cols] + (
-                plain_ref[head, :, cols] + factor[at, :] * scaled_ref[head, :, cols]
-            )
+
+    def body(first):
+        decays, branch_decays = [], []
+        for head in range(heads):
+            at = slice(head, head + 1)
+            if first == 0:
+                decay = jnp.exp(row_ref[:, at] + (late_row_ref[at, :] + after[at, :])) * SCALE
+                decay_ref[head] = decay[:, half:]
+                decays.append(decay[:, :half])
+            else:
+                decays.append(None)
+            branch_decay = jnp.exp(late_branch_ref[head] + after[at, :]) * SCALE
+            branch_decay_ref[head] = branch_decay[:, half:]
+            branch_decays.append(branch_decay[:, :half])
+        sums = half_products(qa_ref, near_ref, first, decays, branch_decays, rows)
+        for head in range(heads):
+            for side in range(2):
+                cols = slice(side * HEAD, (side + 1) * HEAD)
+                sum_ref[head, first:, cols] = sums[head][:, cols] + (
+                    plain_ref[head, first:, cols]
+                    + factor[head : head + 1, :] * scaled_ref[head, first:, cols]
+                )
+
+    needed = late_partner(ctx) < ctx
+    pl.when(needed)(functools.partial(body, 0))
+    pl.when(jnp.logical_not(needed))(functools.partial(body, GROUP * rows))
 
 
 def final_kernel(
-    qa_ref, sum_ref, decay_ref, branch_decay_ref, far_ref, out_ref, branch_ref,
+    late_partner,
+    qa_ref, sum_ref, decay_ref, branch_decay_ref, far_ref, done_ref,
+    out_ref, branch_ref,
     stage_ref, branch_stage_ref, line_ref, sem,
 ):
+    del done_ref
     heads = qa_ref.shape[0]
     rows = out_ref.shape[0]
     owned = branch_ref.shape[0]
     split = GROUP * rows
-    copies = []
-    for head in range(heads):
-        total = sum_ref[head] + half_product(
-            qa_ref[head], far_ref, head, heads, rows, decay_ref[head], branch_decay_ref[head]
-        )
-        ratio = total[:, :HEAD] / jnp.maximum(total[:, HEAD:], 1.0)
-        line_ref[...] = ratio[split:]
+    ctx = lax.axis_index("ctx")
+
+    def branches(head, total):
+        line_ref[head] = total[:, :HEAD] / jnp.maximum(total[:, HEAD:], 1.0)
         for member in range(GROUP):
             column = (head * GROUP + member) * HEAD
-            lanes = slice(column, column + HEAD)
-            stage_ref[:, lanes] = ratio[member * rows : (member + 1) * rows].astype(out_ref.dtype)
-            branch_stage_ref[:, lanes] = line_ref[
-                member * owned : (member + 1) * owned, :
+            branch_stage_ref[:, column : column + HEAD] = line_ref[
+                head, member * owned : (member + 1) * owned, :
             ].astype(branch_ref.dtype)
-        wide = pl.ds(head * GROUP * HEAD, GROUP * HEAD)
-        copies.append(
-            pltpu.make_async_copy(stage_ref.at[:, wide], out_ref.at[:, wide], sem.at[head])
-        )
-        copies[-1].start()
-    copies.append(pltpu.make_async_copy(branch_stage_ref, branch_ref, sem.at[heads]))
-    copies[-1].start()
-    for copy in copies:
-        copy.wait()
+
+    last = pltpu.make_async_copy(branch_stage_ref, branch_ref, sem.at[heads])
+    branch_parts = [branch_decay_ref[head] for head in range(heads)]
+
+    def whole():
+        row_parts = [decay_ref[head] for head in range(heads)]
+        sums = half_products(qa_ref, far_ref, 0, row_parts, branch_parts, rows)
+        for head in range(heads):
+            total = sum_ref[head, :split] + sums[head][:split]
+            put_rows(head, total, stage_ref, out_ref, sem).start()
+            branches(head, sum_ref[head, split:] + sums[head][split:])
+        last.start()
+        for head in range(heads):
+            rows_copy(head, stage_ref, out_ref, sem).wait()
+        last.wait()
+
+    def only_branches():
+        sums = half_products(qa_ref, far_ref, split, [None] * heads, branch_parts, rows)
+        for head in range(heads):
+            branches(head, sum_ref[head, split:] + sums[head])
+        last.start()
+        last.wait()
+
+    needed = late_partner(ctx) < ctx
+    pl.when(needed)(whole)
+    pl.when(jnp.logical_not(needed))(only_branches)
 
 
 def swaps(count):
@@ -328,7 +416,8 @@
 ORDER = (2, 1, 3)
 
 
-def call(kernel, operands, outs, scratch=(), vmem=16 << 20, results=None, inputs=None):
+def call(kernel, operands, outs, scratch=(), vmem=16 << 20, results=None, inputs=None,
+         aliases=None):
     spec = pl.BlockSpec(memory_space=pltpu.VMEM)
     return pl.pallas_call(
         kernel,
@@ -338,6 +427,7 @@
         scratch_shapes=list(scratch),
         compiler_params=pltpu.CompilerParams(vmem_limit_bytes=vmem),
         cost_estimate=pl.CostEstimate(flops=1 << 29, bytes_accessed=4 << 20, transcendentals=0),
+        input_output_aliases=aliases or {},
     )(*operands)
 
 
@@ -396,32 +486,38 @@
         inputs=[hbm] * len(sources),
     )
     early = (count - 1) * length
-    plain, scaled, late_row, late_branch = call(
+    plain, scaled, late_row, late_branch, rows_out = call(
         functools.partial(early_kernel, partners[:-1], partners[-1]),
         [queries_all, acc, token, row_sum, fork, total, *near[:-1], *far[:-1]],
-        (wide, wide, shape((heads, length), f32), shape((heads, padded, length), f32)),
+        (
+            wide, wide, shape((heads, length), f32), shape((heads, padded, length), f32),
+            shape((rows, queries.shape[1]), bf16),
+        ),
         [
-            pltpu.VMEM((total_rows, early), bf16),
-            pltpu.VMEM((total_rows, early), bf16),
-            pltpu.VMEM((early, 2 * HEAD), bf16),
-            pltpu.VMEM((early, HEAD), bf16),
+            pltpu.VMEM((heads, early, 2 * HEAD), bf16),
+            pltpu.VMEM((heads, early, HEAD), bf16),
+            pltpu.VMEM((rows, queries.shape[1]), bf16),
+            pltpu.SemaphoreType.DMA((heads,)),
         ],
+        results=(pl.BlockSpec(memory_space=pltpu.VMEM),) * 4 + (hbm,),
     )
     sums, decay, branch_decay = call(
-        near_kernel,
+        functools.partial(near_kernel, partners[-1]),
         [queries_all, row_sum, plain, scaled, late_row, late_branch, near[-1]],
         (wide, shape((heads, rows, half), f32), shape((heads, padded, half), f32)),
     )
     return call(
-        final_kernel, [queries_all, sums, decay, branch_decay, far[-1]],
+        functools.partial(final_kernel, partners[-1]),
+        [queries_all, sums, decay, branch_decay, far[-1], in_hbm(rows_out)],
         (shape((rows, queries.shape[1]), bf16), shape((owned, queries.shape[1]), bf16)),
         [
             pltpu.VMEM((rows, queries.shape[1]), bf16),
             pltpu.VMEM((owned, queries.shape[1]), bf16),
-            pltpu.VMEM((padded, HEAD), f32),
+            pltpu.VMEM((heads, padded, HEAD), f32),
             pltpu.SemaphoreType.DMA((heads + 1,)),
         ],
-        results=(hbm, hbm),
+        results=(hbm, hbm), inputs=[pl.BlockSpec(memory_space=pltpu.VMEM)] * 5 + [hbm],
+        aliases={5: 0},
     )
 
 

time: 23.5 us -> 23.4 us (level)
  transfers between devices with their start and end apart: 6 -> 6, of which waited for: 2 -> 2; matrix products, arithmetic and copies ran while one was open for 0% -> 0% of each run, Pallas kernels for 20% -> 21%
where the time goes in v4:
time: 23.4 us; the launch traced here: 23.2 us
  waiting for transfers between devices  7.79 us (33%)
  starting transfers between devices  7.69 us (33%)
  Pallas kernels  7.04 us (30%)
  between operations  0.7 us (3%)
    ppermute x3, waiting for transfers between devices, per_device(): near.append(lax.ppermute(payload, 'ctx', pairings[s][0]))  7.78 us
    pallas_call x5, Pallas kernels, call(): pl.pallas_call(kernel, out_shape=outs, in_specs=inputs or [spec] * len(op...  7.04 us
    ppermute x3, starting transfers between devices, per_device(): far.append(lax.ppermute(part, 'feat', [(0, 1), (1, 0)]))  4.98 us
    ppermute x3, starting transfers between devices, per_device(): near.append(lax.ppermute(payload, 'ctx', pairings[s][0]))  2.71 us
  transfers between devices with their start and end apart: 6, of which 2 were waited for; matrix products, arithmetic and copies ran while one was open for 0% of the time, Pallas kernels for 21%

profile of v4, /device:TPU:17, one launch (start us, length us, event | category | flops | bytes accessed | tf_op | source)
XLA Modules:
  0.0 23.2 jit_solution(16147804165437826477)
XLA Ops:
  0.6 0.9 %shard_map.105 = bf16[520,128]{1,0:T(8,128)(2,1)S(1)} custom-call(bf16[128,512]{1,0:T(8,128)(2,1)} %k_ref.1, bf16[128,512]{1,0:T(8,128)(2,1)} %v_ref.1, f32[4,128]{1,0:T(4,128)} %bitcast.4), custom_call_target="tpu_custom_call" | custom-call | flops 536870912 | bytes 4194304 | tf_op jit(solution)/shard_map/pallas_call | solution.py:422
  1.6 0.1 collective-permute-start
  1.6 1.4 %collective-permute-start.1 = (bf16[520,128]{1,0:T(8,128)(2,1)S(1)}, bf16[520,128]{1,0:T(8,128)(2,1)S(1)}, u32[]{:S(2)}, u32[]{:S(2)}) collective-permute-start(bf16[520,128]{1,0:T(8,128)(2,1)S(1)} %shard_map.105), channel_id=1, source_target_pairs={{0,4},{4,0},{8,12},{12,8},{1,5},{5,1},{9,13},{13,9},{2,6},{6,2},{1... | collective-permute-start | bytes 399368 | tf_op jit(solution)/shard_map/ppermute | solution.py:463
  3.0 1.3 %collective-permute-start.4 = (bf16[520,128]{1,0:T(8,128)(2,1)S(1)}, bf16[520,128]{1,0:T(8,128)(2,1)S(1)}, u32[]{:S(2)}, u32[]{:S(2)}) collective-permute-start(bf16[520,128]{1,0:T(8,128)(2,1)S(1)} %shard_map.105), channel_id=1, source_target_pairs={{0,12},{4,8},{8,4},{12,0},{1,13},{5,9},{9,5},{13,1},{2,14},{6,10},... | collective-permute-start | bytes 399368 | tf_op jit(solution)/shard_map/ppermute | solution.py:463
  4.3 2.7 %collective-permute-done.refs_6_ = bf16[520,128]{1,0:T(8,128)(2,1)S(1)} collective-permute-done((bf16[520,128]{1,0:T(8,128)(2,1)S(1)}, bf16[520,128]{1,0:T(8,128)(2,1)S(1)}, u32[]{:S(2)}, u32[]{:S(2)}) %collective-permute-start) | collective-permute-done | bytes 133152 | tf_op jit(solution)/shard_map/ppermute | solution.py:463
  7.0 2.7 %collective-permute-start.2 = (bf16[520,128]{1,0:T(8,128)(2,1)S(1)}, bf16[520,128]{1,0:T(8,128)(2,1)S(1)}, u32[]{:S(2)}, u32[]{:S(2)}) collective-permute-start(bf16[520,128]{1,0:T(8,128)(2,1)S(1)} %collective-permute-done.refs_6_), channel_id=1, source_target_pairs={{0,1},{1,0},{2,3},{3,2},{4,5},{5,4},{6,7},{7,6},{8,9},{9,8},{10,11... | collective-permute-start | bytes 399368 | tf_op jit(solution)/shard_map/ppermute | solution.py:465
  9.6 0.0 collective-permute-done.1.refs_7_
  9.6 1.8 %collective-permute-start.3 = (bf16[520,128]{1,0:T(8,128)(2,1)S(1)}, bf16[520,128]{1,0:T(8,128)(2,1)S(1)}, u32[]{:S(2)}, u32[]{:S(2)}) collective-permute-start(bf16[520,128]{1,0:T(8,128)(2,1)S(1)} %collective-permute-done.1.refs_7_), channel_id=1, source_target_pairs={{0,1},{1,0},{2,3},{3,2},{4,5},{5,4},{6,7},{7,6},{8,9},{9,8},{10,11... | collective-permute-start | bytes 399368 | tf_op jit(solution)/shard_map/ppermute | solution.py:465
  11.5 5.1 %collective-permute-done.4.near_ref = bf16[520,128]{1,0:T(8,128)(2,1)S(1)} collective-permute-done((bf16[520,128]{1,0:T(8,128)(2,1)S(1)}, bf16[520,128]{1,0:T(8,128)(2,1)S(1)}, u32[]{:S(2)}, u32[]{:S(2)}) %collective-permute-start.4) | collective-permute-done | bytes 133152 | tf_op jit(solution)/shard_map/ppermute | solution.py:463
  16.6 0.5 %collective-permute-start.5 = (bf16[520,128]{1,0:T(8,128)(2,1)S(1)}, bf16[520,128]{1,0:T(8,128)(2,1)S(1)}, u32[]{:S(2)}, u32[]{:S(2)}) collective-permute-start(bf16[520,128]{1,0:T(8,128)(2,1)S(1)} %collective-permute-done.4.near_ref), channel_id=1, source_target_pairs={{0,1},{1,0},{2,3},{3,2},{4,5},{5,4},{6,7},{7,6},{8,9},{9,8},{10,11... | collective-permute-start | bytes 399368 | tf_op jit(solution)/shard_map/ppermute | solution.py:465
  17.1 2.8 %shard_map.104 = (bf16[4,336,128]{2,1,0:T(8,128)(2,1)S(1)}, f32[4,336,256]{2,1,0:T(8,128)S(1)}, f32[4,16,256]{2,1,0:T(8,128)S(1)}, f32[64,4]{1,0:T(8,128)S(1)}, ...) custom-call(bf16[128,2560]{1,0:T(8,128)(2,1)} %refs_0_.1, bf16[128,512]{1,0:T(8,128)(2,1)} %k_ref.1, bf16[128,512]{1,0:T(8,128)(2,1)} %v_ref.1, ...), custom_call_target="tpu_custom_call" | custom-call | flops 536870912 | bytes 4194304 | tf_op jit(solution)/shard_map/pallas_call | solution.py:422
  19.8 0.0 collective-permute-done.2.refs_8_
  19.8 0.0 collective-permute-done.3.refs_9_
  19.9 1.3 %shard_map.106 = (f32[4,336,256]{2,1,0:T(8,128)S(1)}, f32[4,336,256]{2,1,0:T(8,128)S(1)}, f32[4,128]{1,0:T(4,128)S(1)}, f32[4,16,128]{2,1,0:T(8,128)S(1)}, bf16[64,2560]{1,0:T(8,128)(2,1)}) custom-call(bf16[4,336,128]{2,1,0:T(8,128)(2,1)S(1)} %get-tuple-element.16.refs_0_.qa_ref, f32[4,336,256]{2,1,0:T(8,128)S(1)} %get-tuple-element.18.refs_1_, ...), custom_call_target="tpu_custom_call" | custom-call | flops 536870912 | bytes 4194304 | tf_op jit(solution)/shard_map/pallas_call | solution.py:422
  21.1 0.8 %shard_map.107 = (f32[4,336,256]{2,1,0:T(8,128)S(1)}, f32[4,64,64]{2,1,0:T(8,128)S(1)}, f32[4,16,64]{2,1,0:T(8,128)S(1)}) custom-call(bf16[4,336,128]{2,1,0:T(8,128)(2,1)S(1)} %get-tuple-element.16.refs_0_.qa_ref, f32[64,4]{1,0:T(8,128)S(1)} %get-tuple-element.17.refs_3_.row_ref, f32[4,336,256]{2,1,0:T(8,128)S(1)} %get-tuple-element.22.plain_ref, ...), custom_call_target="tpu_custom_call" | custom-call | flops 536870912 | bytes 4194304 | tf_op jit(solution)/shard_map/pallas_call | solution.py:422
  21.9 0.0 collective-permute-done.5.far_ref
  22.0 1.2 %shard_map.108 = (bf16[64,2560]{1,0:T(8,128)(2,1)}, bf16[2,2560]{1,0:T(2,128)(2,1)}) custom-call(bf16[4,336,128]{2,1,0:T(8,128)(2,1)S(1)} %get-tuple-element.16.refs_0_.qa_ref, f32[4,336,256]{2,1,0:T(8,128)S(1)} %get-tuple-element.26.sum_ref, f32[4,64,64]{2,1,0:T(8,128)S(1)} %get-tuple-element.27.decay_ref, ...), custom_call_target="tpu_custom_call", output_to_operand_aliasing={{0}: (5, {})} | custom-call | flops 536870912 | bytes 4194304 | tf_op jit(solution)/shard_map/pallas_call | solution.py:422
Async XLA Ops:
  1.6 5.4 %collective-permute-start = (bf16[520,128]{1,0:T(8,128)(2,1)S(1)}, bf16[520,128]{1,0:T(8,128)(2,1)S(1)}, u32[]{:S(2)}, u32[]{:S(2)}) collective-permute-start(bf16[520,128]{1,0:T(8,128)(2,1)S(1)} %shard_map.105), channel_id=1, source_target_pairs={{0,8},{4,12},{8,0},{12,4},{1,9},{5,13},{9,1},{13,5},{2,10},{6,14},... | collective-permute-start | bytes 399368 | tf_op jit(solution)/shard_map/ppermute | solution.py:463
  1.6 8.0 %collective-permute-start.1 = (bf16[520,128]{1,0:T(8,128)(2,1)S(1)}, bf16[520,128]{1,0:T(8,128)(2,1)S(1)}, u32[]{:S(2)}, u32[]{:S(2)}) collective-permute-start(bf16[520,128]{1,0:T(8,128)(2,1)S(1)} %shard_map.105), channel_id=1, source_target_pairs={{0,4},{4,0},{8,12},{12,8},{1,5},{5,1},{9,13},{13,9},{2,6},{6,2},{1... | collective-permute-start | bytes 399368 | tf_op jit(solution)/shard_map/ppermute | solution.py:463
  3.0 13.5 %collective-permute-start.4 = (bf16[520,128]{1,0:T(8,128)(2,1)S(1)}, bf16[520,128]{1,0:T(8,128)(2,1)S(1)}, u32[]{:S(2)}, u32[]{:S(2)}) collective-permute-start(bf16[520,128]{1,0:T(8,128)(2,1)S(1)} %shard_map.105), channel_id=1, source_target_pairs={{0,12},{4,8},{8,4},{12,0},{1,13},{5,9},{9,5},{13,1},{2,14},{6,10},... | collective-permute-start | bytes 399368 | tf_op jit(solution)/shard_map/ppermute | solution.py:463
  7.0 12.9 %collective-permute-start.2 = (bf16[520,128]{1,0:T(8,128)(2,1)S(1)}, bf16[520,128]{1,0:T(8,128)(2,1)S(1)}, u32[]{:S(2)}, u32[]{:S(2)}) collective-permute-start(bf16[520,128]{1,0:T(8,128)(2,1)S(1)} %collective-permute-done.refs_6_), channel_id=1, source_target_pairs={{0,1},{1,0},{2,3},{3,2},{4,5},{5,4},{6,7},{7,6},{8,9},{9,8},{10,11... | collective-permute-start | bytes 399368 | tf_op jit(solution)/shard_map/ppermute | solution.py:465
  9.6 10.2 %collective-permute-start.3 = (bf16[520,128]{1,0:T(8,128)(2,1)S(1)}, bf16[520,128]{1,0:T(8,128)(2,1)S(1)}, u32[]{:S(2)}, u32[]{:S(2)}) collective-permute-start(bf16[520,128]{1,0:T(8,128)(2,1)S(1)} %collective-permute-done.1.refs_7_), channel_id=1, source_target_pairs={{0,1},{1,0},{2,3},{3,2},{4,5},{5,4},{6,7},{7,6},{8,9},{9,8},{10,11... | collective-permute-start | bytes 399368 | tf_op jit(solution)/shard_map/ppermute | solution.py:465
  16.6 5.4 %collective-permute-start.5 = (bf16[520,128]{1,0:T(8,128)(2,1)S(1)}, bf16[520,128]{1,0:T(8,128)(2,1)S(1)}, u32[]{:S(2)}, u32[]{:S(2)}) collective-permute-start(bf16[520,128]{1,0:T(8,128)(2,1)S(1)} %collective-permute-done.4.near_ref), channel_id=1, source_target_pairs={{0,1},{1,0},{2,3},{3,2},{4,5},{5,4},{6,7},{7,6},{8,9},{9,8},{10,11... | collective-permute-start | bytes 399368 | tf_op jit(solution)/shard_map/ppermute | solution.py:465
